TPU v7x, 512 devices: a whole 4x4x16 slice. The times are simulated.
512 devices in a mesh: dp: 128 (over y, z, core), tensor: 4 (over x).
Axes of the slice: x: 4, y: 4, z: 16, core: 2. Of those that a mesh axis runs over, the one named last changes fastest.
Arguments:
- acts: bfloat16 [8, 32768, 2048], P(None, 'dp', 'tensor'), may hold values from -24 to 24
- out_cot: bfloat16 [8, 32768, 1024], P(None, 'dp', 'tensor'), may hold values from -24 to 24
- emb_ids: int32 [32768], P(('dp', 'tensor')), may hold values from 0 to 8191
- emb_cot: bfloat16 [32768, 1024], P('dp', 'tensor'), may hold values from -24 to 24
- grad_w: float32 [8192, 2048], P(('dp', 'tensor')), may hold values from -6 to 6
- grad_e: float32 [8192, 1024], P(('dp', 'tensor')), may hold values from -6 to 6
Outputs:
- update_w: float32 [8192, 2048], P('dp', 'tensor')
- update_e: float32 [8192, 1024], P(('dp', 'tensor'))
All inputs are finite; a program needn't handle non-finite values. Where the computation divides by a largest or mean magnitude, that divisor is 1e-20 or more.
Results may differ from a plain program's by a relative error of at most 0.0003.
Values sent between devices are 32-bit elements; how exact they have to be, the bound alone decides.
A program may use at most 64 MiB of HBM per device.

v0:
```python
import jax
import jax.numpy as jnp
from jax import lax
from jax.sharding import PartitionSpec as P

HEAD = 64
NS_ITERS = 4


damp_root = 0.7


def newton_inverse(matrices):
    size = matrices.shape[-1]
    eye = jnp.eye(size, dtype=jnp.float32)
    bound = jnp.max(jnp.sum(jnp.abs(matrices), axis=-1), axis=-1)
    approx = eye[None] / bound[:, None, None]
    for sweep in range(NS_ITERS):
        image = jnp.einsum("bij,bjk->bik", matrices, approx, precision=lax.Precision.HIGHEST)
        approx = jnp.einsum(
            "bij,bjk->bik", approx, 2.0 * eye[None] - image, precision=lax.Precision.HIGHEST
        )
    return approx


def local(acts, out_cot, emb_ids, emb_cot, grad_w, grad_e):
    n_dp = lax.axis_size("dp")
    n_tp = lax.axis_size("tensor")
    layers, tok_rows, inner_part = acts.shape
    width_part = out_cot.shape[2]
    heads_part = inner_part // HEAD
    groups_part = width_part // HEAD
    tokens_all = tok_rows * n_dp
    width = width_part * n_tp
    inner = inner_part * n_tp
    groups_all = width // HEAD
    rows_e = grad_e.shape[0]
    vocab = rows_e * n_dp * n_tp
    dp_index = lax.axis_index("dp")
    flat_index = dp_index * n_tp + lax.axis_index("tensor")
    tile_rows = grad_w.shape[0] * n_tp
    block_rows = tile_rows // HEAD
    layer_rows = min(tile_rows, width)
    layer_span = tile_rows // layer_rows
    first_layer = dp_index * tile_rows // width
    split_acts = acts.reshape(layers, tok_rows, heads_part, HEAD)
    gram_a = jnp.einsum(
        "lthi,lthj->lhij", split_acts, split_acts, preferred_element_type=jnp.float32
    )
    split_cot = out_cot.reshape(layers, tok_rows, groups_part, HEAD)
    gram_g = jnp.einsum("lthi,lthj->lhij", split_cot, split_cot, preferred_element_type=jnp.float32)
    split_emb = emb_cot.reshape(tok_rows, groups_part, HEAD)
    gram_e = jnp.einsum("thi,thj->hij", split_emb, split_emb, preferred_element_type=jnp.float32)
    blocks = jnp.concatenate(
        [gram_a.reshape(-1, HEAD, HEAD), gram_g.reshape(-1, HEAD, HEAD), gram_e], axis=0
    )
    block_count = blocks.shape[0]
    diagonal_sums = jnp.trace(blocks, axis1=1, axis2=2)
    local_a = jnp.sum(diagonal_sums[: layers * heads_part].reshape(layers, heads_part), axis=1)
    local_g = jnp.sum(
        diagonal_sums[layers * heads_part : layers * (heads_part + groups_part)].reshape(
            layers, groups_part
        ),
        axis=1,
    )
    local_e = jnp.sum(diagonal_sums[layers * (heads_part + groups_part) :])
    trace_local = jnp.concatenate([local_a, local_g, local_e[None]])
    local_counts = jnp.sum(
        (emb_ids[:, None] == jnp.arange(vocab, dtype=jnp.int32)[None, :]).astype(jnp.float32),
        axis=0,
    )
    traces, counts_all = lax.psum((trace_local, local_counts), ("dp", "tensor"))
    counts_mine = lax.dynamic_slice_in_dim(counts_all, flat_index * rows_e, rows_e)
    trace_a = traces[:layers]
    trace_g = traces[layers : 2 * layers]
    trace_e = traces[2 * layers]
    ratio = jnp.sqrt(trace_a / (tokens_all * inner) / (trace_g / (tokens_all * width)))
    ratio_e = jnp.sqrt(tokens_all / vocab / (trace_e / (tokens_all * width)))
    shift = jnp.concatenate(
        [
            jnp.repeat(damp_root * ratio, heads_part),
            jnp.repeat(damp_root / ratio, groups_part),
            jnp.full((groups_part,), 1.0, jnp.float32) * (damp_root / ratio_e),
        ]
    )
    eye = jnp.eye(HEAD, dtype=jnp.float32)
    owned = -(-block_count // n_dp)
    slots = owned * n_dp
    padded = jnp.pad(blocks.reshape(block_count, HEAD * HEAD), ((0, slots - block_count), (0, 0)))
    mine = lax.psum_scatter(padded, "dp", scatter_dimension=0, tiled=True)
    shift_pad = jnp.pad(shift, (0, slots - block_count), constant_values=1.0)
    shift_mine = lax.dynamic_slice_in_dim(shift_pad, dp_index * owned, owned)
    damped = mine.reshape(owned, HEAD, HEAD) / tokens_all + shift_mine[:, None, None] * eye
    inverse_mine = newton_inverse(damped)
    gathered = lax.all_gather(inverse_mine.reshape(owned, HEAD * HEAD), "dp", axis=0, tiled=True)
    inverses = gathered[:block_count].reshape(block_count, HEAD, HEAD)
    inv_a = inverses[: layers * heads_part].reshape(layers, heads_part, HEAD, HEAD)
    inv_g_part = inverses[layers * heads_part : layers * (heads_part + groups_part)].reshape(
        layers, groups_part, HEAD * HEAD
    )
    inv_e_part = inverses[layers * (heads_part + groups_part) :].reshape(groups_part, HEAD * HEAD)
    base_layer = 0
    sending = jnp.concatenate(
        [inv_g_part.reshape(layers * groups_part, HEAD * HEAD), inv_e_part], axis=0
    )
    shared = lax.all_gather(sending[None], "tensor", axis=0, tiled=True)
    inv_g = shared[:, : layers * groups_part].reshape(n_tp, layers, groups_part, HEAD, HEAD)
    inv_g = jnp.transpose(inv_g, (1, 0, 2, 3, 4)).reshape(layers * groups_all, HEAD, HEAD)
    inv_e = shared[:, layers * groups_part :].reshape(groups_all, HEAD, HEAD)
    tile = lax.all_to_all(grad_w, "tensor", split_axis=1, concat_axis=0, tiled=True)
    g_sel = lax.dynamic_slice_in_dim(
        inv_g, dp_index * block_rows - base_layer * groups_all, block_rows, 0
    )
    left = jnp.einsum(
        "bij,bjc->bic",
        g_sel,
        tile.reshape(block_rows, HEAD, inner_part),
        precision=lax.Precision.HIGHEST,
    )
    a_sel = lax.dynamic_slice_in_dim(inv_a, first_layer, layer_span, 0)
    right = jnp.einsum(
        "lrhi,lhij->lrhj",
        left.reshape(layer_span, layer_rows, heads_part, HEAD),
        a_sel,
        precision=lax.Precision.HIGHEST,
    )
    update_w = right.reshape(tile_rows, inner_part)
    scaled = jnp.einsum(
        "rgi,gij->rgj",
        grad_e.reshape(rows_e, groups_all, HEAD),
        inv_e,
        precision=lax.Precision.HIGHEST,
    )
    update_e = scaled.reshape(rows_e, width) / (counts_mine + damp_root * ratio_e)[:, None]
    return (update_w, update_e)


def solution(mesh):
    in_specs = (
        P(None, "dp", "tensor"),
        P(None, "dp", "tensor"),
        P(("dp", "tensor")),
        P("dp", "tensor"),
        P(("dp", "tensor"), None),
        P(("dp", "tensor"), None),
    )
    out_specs = (P("dp", "tensor"), P(("dp", "tensor"), None))
    return jax.shard_map(local, mesh=mesh, in_specs=in_specs, out_specs=out_specs, check_vma=False)
```

profile of v0, /device:TPU:1, one launch (start us, length us, event | category | flops | bytes accessed | tf_op | source)
XLA Modules:
  0.0 588.8 jit_solution(13494018394217157497)
XLA Ops:
  7.2 3.9 copy.48
  11.1 3.0 fusion.24
  14.2 1.3 copy.49
  15.5 2.0 fusion.25
  17.8 1.6 concatenate.21
  19.4 1.1 concatenate.22
  20.7 2.9 select_maximum_fusion
  26.7 112.1 %all-reduce.3 = (f32[17]{0:T(128)S(1)}, f32[8192]{0:T(1024)S(1)}) all-reduce(f32[17]{0:T(128)S(1)} %pad_maximum_fusion, f32[8192]{0:T(1024)S(1)} %convert_reduce_fusion), channel_id=1, replica_groups=mesh['dp'=128,'tensor'=4] {'dp','tensor'}, use_global_device_ids=true, to_apply=%region_5.6 | all-reduce | flops 8209 | bytes 65672 | tf_op jit(solution)/shard_map/psum | solution.py:72
  142.0 1.3 dynamic-slice
  143.3 237.0 %all-reduce.6.cloned.1.call-done = f32[128,4096]{1,0:T(8,128)} async-done(((f32[128,4096]{1,0:T(8,128)}), f32[128,4096]{1,0:T(8,128)}) %all-reduce.6.cloned.1.call-update) | async-done | bytes 2097168
  380.8 2.3 add_reduce_fusion
  388.1 139.9 %all-gather.6.cloned.1.call-done = f32[128,1,4096]{2,1,0:T(1,128)} async-done(((f32[1,1,4096]{2,1,0:T(1,128)}), f32[128,1,4096]{2,1,0:T(1,128)}) %all-gather.6.cloned.1.call-update) | async-done | bytes 2097168 | tf_op jit(solution)/shard_map/all_gather | solution.py:95
  528.0 1.3 slice_bitcast_fusion
  529.3 1.2 copy.52
  531.2 4.0 all-to-all-start
  535.3 4.7 all-to-all-done
  540.1 2.7 slice_reduce_fusion
  542.8 2.2 reshape.272
  545.0 24.2 %all-gather.8.cloned.1.call-done = f32[4,36,4096]{2,1,0:T(8,128)} async-done(((f32[1,36,4096]{2,1,0:T(8,128)}), f32[4,36,4096]{2,1,0:T(8,128)}) %all-gather.8.cloned.1.call-update) | async-done | bytes 2359312 | tf_op jit(solution)/shard_map/all_gather | solution.py:106
  569.1 1.1 slice.59
  571.2 1.6 slice-done
  572.8 3.0 reshape.274
  575.8 2.5 copy.53
  579.2 1.6 fusion.1
  (70 shorter events, 15.0 us)
Async XLA Ops:
  7.2 373.2 %all-reduce.6.cloned.1.call-start = ((), (), s32[]{:S(2)}) async-start(), calls=%async_computation.3 | async-start | bytes 4194304
  11.1 3.0 copy-start.1
  15.5 2.0 copy-start.2
  23.6 2.1 copy-start.5
  23.6 504.4 %all-gather.6.cloned.1.call-start = ((), (), s32[]{:S(2)}) async-start(), calls=%async_computation.1 | async-start | bytes 2113536 | tf_op jit(solution)/shard_map/all_gather | solution.py:95
  142.0 388.5 %copy-start.3 = (f32[16,2048]{1,0:T(8,128)S(1)}, f32[16,2048]{1,0:T(8,128)}, u32[]{:S(2)}) copy-start(f32[16,2048]{1,0:T(8,128)} %param.10) | copy-start | bytes 393220
  386.5 148.6 %copy-start.4 = (f32[16,1024]{1,0:T(8,128)S(1)}, f32[16,1024]{1,0:T(8,128)}, u32[]{:S(2)}) copy-start(f32[16,1024]{1,0:T(8,128)} %param.11) | copy-start | bytes 196612
  388.1 181.0 %all-gather.8.cloned.1.call-start = ((), (), s32[]{:S(2)}) async-start(), calls=%async_computation.2 | async-start | bytes 3276800 | tf_op jit(solution)/shard_map/all_gather | solution.py:106
  528.0 12.1 %copy-start = (f32[128,1,4096]{2,1,0:T(1,128)S(1)}, f32[128,1,4096]{2,1,0:T(1,128)}, u32[]{:S(2)}) copy-start(f32[128,1,4096]{2,1,0:T(1,128)} %all-gather.6.cloned.1.call-done) | copy-start | bytes 6291460
  531.2 8.8 %all-to-all-start = ((f32[16,4,512]{2,0,1:T(8,128)}), f32[16,4,512]{2,0,1:T(8,128)S(1)}, u32[]{:S(2)}, u32[]{:S(2)}) async-start(f32[16,4,512]{2,0,1:T(8,128)} %bitcast.65), calls=%async_computation | async-start | bytes 262144 | tf_op jit(solution)/shard_map/all_to_all | solution.py:110
  571.2 1.6 slice-start
Sparse Core Ops, SparseCore 0:
  23.7 356.5 all-reduce.5
  388.2 139.7 all-gather.5
  530.6 38.4 all-gather.7
where the time goes:
time: 589 us
  waiting for transfers between devices  406 us (69%)
  blocking collectives  112 us (19%)
  local copies, waits for them, and re-layouts  30.4 us (5%)
  between operations  15.5 us (3%)
  other arithmetic  11 us (2%)
  matrix products  10.1 us (2%)
    unnamed x4, waiting for transfers between devices  237 us
    all_gather x1, waiting for transfers between devices, local(): lax.all_gather(inverse_mine.reshape(owned, HEAD * HEAD), 'dp', axis=0, ti...  140 us
    psum x1, blocking collectives, local(): traces, counts_all = lax.psum((trace_local, local_counts), ('dp', 'tensor'))  112 us
    all_gather x1, waiting for transfers between devices, local(): shared = lax.all_gather(sending[None], 'tensor', axis=0, tiled=True)  24.2 us
  transfers between devices with their start and end apart: 4, of which 4 were waited for; matrix products, arithmetic and copies ran while one was open for 2% of the time, Pallas kernels for 0%

commit v1 on v0

v1 whole, which is shorter than its diff:
```python
import jax
import jax.numpy as jnp
from jax import lax
from jax.experimental import pallas as pl
from jax.experimental.pallas import tpu as pltpu
from jax.sharding import PartitionSpec as P

HEAD = 64
NS_ITERS = 4
DAMP = 0.7
LAYERS = 8
TOKENS = 32768
VOCAB = 8192
WIDTH = 1024
INNER = 2048
NX, NY, NZ = 4, 4, 16
MESH = pl.DeviceIdType.MESH
F32 = jnp.float32
HI = lax.Precision.HIGHEST
HOLD = (2, 5, 0)


def coords():
    d = lax.axis_index("dp").astype(jnp.int32)
    x = lax.axis_index("tensor").astype(jnp.int32)
    c = lax.rem(d, 2)
    z = lax.rem(lax.div(d, 2), NZ)
    y = lax.div(d, 2 * NZ)
    return x, y, z, c


def dev(x, y, z, c):
    return ((y * NZ + z) * 2 + c, x)


def send(src, dst, send_sem, recv_sem, device):
    return pltpu.make_async_remote_copy(
        src_ref=src, dst_ref=dst, send_sem=send_sem, recv_sem=recv_sem, device_id=device, device_id_type=MESH
    )


def loop(low, high, body):
    def step(k, carry):
        body(k)
        return carry

    lax.fori_loop(low, high, step, 0)


def pair_of(product):
    lane = lax.broadcasted_iota(jnp.int32, (HEAD, 2 * HEAD), 1)
    return jnp.where(lane < HEAD, product[:HEAD], product[HEAD:])


def blockdiag(pair):
    lane = lax.broadcasted_iota(jnp.int32, (HEAD, 2 * HEAD), 1)
    zero = jnp.zeros_like(pair)
    return jnp.concatenate([jnp.where(lane < HEAD, pair, zero), jnp.where(lane < HEAD, zero, pair)], axis=0)


def gram_kernel(acts, cot, emb, ids_row, ids_col, blk, eblk, m):
    lane = lax.broadcasted_iota(jnp.int32, (HEAD, 2 * HEAD), 1)
    row = lax.broadcasted_iota(jnp.int32, (HEAD, 2 * HEAD), 0)
    on_diag = (lane == row) | (lane == row + HEAD)

    def gram(x):
        full = lax.dot_general(x, x, (((0,), (0,)), ((), ())), preferred_element_type=F32)
        pair = pair_of(full)
        return pair, jnp.sum(jnp.where(on_diag, pair, 0.0), axis=0, keepdims=True)

    ids_r = ids_row[...]
    ids_c = ids_col[...]
    hit_row = (lax.broadcasted_iota(jnp.int32, (64, 64), 0) == lax.shift_right_logical(ids_r, 7)).astype(F32)
    hit_lane = (lax.broadcasted_iota(jnp.int32, (64, 128), 1) == (ids_c & 127)).astype(F32)
    hist = jnp.dot(hit_row.astype(jnp.bfloat16), hit_lane.astype(jnp.bfloat16), preferred_element_type=F32)
    sum_e = jnp.zeros((1, 128), F32)
    for core in range(2):
        pair, diag = gram(emb[:, 128 * core : 128 * core + 128])
        eblk[core] = pair
        sum_e = sum_e + diag
    rows = {}
    for layer in range(LAYERS):
        sum_a = jnp.zeros((1, 128), F32)
        sum_g = jnp.zeros((1, 128), F32)
        for core in range(2):
            for p in range(2):
                q = 2 * core + p
                pair, diag = gram(acts[layer, :, 128 * q : 128 * q + 128])
                blk[core, 3 * layer + p] = pair
                sum_a = sum_a + diag
            pair, diag = gram(cot[layer, :, 128 * core : 128 * core + 128])
            blk[core, 3 * layer + 2] = pair
            sum_g = sum_g + diag
        rows[layer] = (sum_a, sum_g)
    for y in range(NY):
        m[y, 0:16] = hist[16 * y : 16 * y + 16]
        tail = [rows[2 * y][0], rows[2 * y + 1][0], rows[2 * y][1], rows[2 * y + 1][1], sum_e]
        m[y, 16:24] = jnp.concatenate(tail + [jnp.zeros((3, 128), F32)], axis=0)


def reduce_kernel(
    blk, eblk, m, gw, own_o, e_o, tr_o, tile_o,
    rblk, reb, rm, s1, se, ms, nz, ec, ef, s2, ry, re, rmm, rey, rz, rn, eag, rt,
    c_s, c_r, y_s, y_r, e_s, e_r, m_s, m_r, ey_s, ey_r, z_s, z_r, n_s, n_r, g_s, g_r, t_s, t_r,
):
    x, y, z, c = coords()
    h = lax.div(z, 8)
    other = dev(x, y, z, 1 - c)

    def at_xy(k):
        return lax.rem(x + lax.div(k, 4), 4), lax.rem(y + lax.rem(k, 4), 4)

    def at_z(k):
        return dev(x, y, lax.rem(z + k, NZ), c)

    def at_y(k):
        return dev(x, lax.rem(y + k, NY), z, c)

    def at_x(k):
        return dev(lax.rem(x + k, NX), y, z, c)

    barrier = pltpu.get_barrier_semaphore()
    pl.semaphore_signal(barrier, inc=1, device_id=other, device_id_type=MESH)

    def greet_xy(k):
        xx, yy = at_xy(k)
        pl.semaphore_signal(barrier, inc=1, device_id=dev(xx, yy, z, c), device_id_type=MESH)

    def greet_z(k):
        pl.semaphore_signal(barrier, inc=1, device_id=at_z(k), device_id_type=MESH)

    loop(1, 16, greet_xy)
    loop(1, 16, greet_z)
    pl.semaphore_wait(barrier, 31)

    def core_chunk(i):
        k = (2, 1, 3, 0)[i]
        yy = lax.rem(y + k, NY)
        part = pl.ds(6 * yy, 6)
        return send(blk.at[1 - c, part], rblk.at[part], c_s.at[i], c_r.at[i], other)

    e_core = send(eblk.at[1 - c], reb, c_s.at[4], c_r.at[4], other)
    m_core = send(m, rm, c_s.at[5], c_r.at[5], other)
    e_core.start()
    m_core.start()
    for i in range(4):
        core_chunk(i).start()

    def g_copy(k):
        cols = pl.ds(pl.multiple_of(lax.rem(x + k, NX) * 512, 512), 512)
        return send(gw.at[:, cols], rt.at[k], t_s.at[k], t_r.at[k], at_x(k))

    def g_start(k):
        g_copy(k).start()

    loop(1, NX, g_start)

    e_core.wait_recv()
    e_sum = eblk[c] + reb[...]
    for k in range(NZ):
        se[k] = e_sum[4 * k : 4 * k + 4]

    def e_copy(k):
        return send(se.at[lax.rem(z + k, NZ)], re.at[k], e_s.at[k], e_r.at[k], at_z(k))

    def e_start(k):
        e_copy(k).start()

    loop(1, NZ, e_start)
    m_core.wait_recv()
    for k in range(NY):
        ms[k] = m[k] + rm[k]

    def m_copy(k):
        xx, yy = at_xy(k)
        return send(ms.at[yy], rmm.at[k], m_s.at[k], m_r.at[k], dev(xx, yy, z, c))

    def m_start(k):
        m_copy(k).start()

    loop(1, 16, m_start)

    def y_copy(k):
        part = pl.ds(6 * lax.rem(y + k, NY), 6)
        return send(s1.at[part], ry.at[k], y_s.at[k], y_r.at[k], at_y(k))

    for i in range(4):
        k = (2, 1, 3, 0)[i]
        core_chunk(i).wait_recv()
        first = 6 * lax.rem(y + k, NY)

        def add(j, first=first):
            s1[first + j] = blk[c, first + j] + rblk[first + j]

        loop(0, 6, add)
        if k:
            y_copy(k).start()

    def e_add(k, total):
        e_copy(k).wait_recv()
        return total + re[k]

    ec[...] = lax.fori_loop(1, NZ, e_add, se[z])

    def ey_copy(k):
        return send(ec, rey.at[k], ey_s.at[k], ey_r.at[k], at_y(k))

    def ey_start(k):
        ey_copy(k).start()

    loop(1, NY, ey_start)

    def m_add(k, total):
        m_copy(k).wait_recv()
        return total + rmm[k]

    n = lax.fori_loop(1, 16, m_add, ms[y])
    for k in range(NZ):
        nz[k] = jnp.concatenate([n[k : k + 1], n[16:23]], axis=0)

    def n_copy(k):
        return send(nz.at[lax.rem(z + k, NZ)], rn.at[k], n_s.at[k], n_r.at[k], at_z(k))

    def n_start(k):
        n_copy(k).start()

    loop(1, NZ, n_start)

    def ey_add(k, total):
        ey_copy(k).wait_recv()
        return total + rey[k]

    ef[...] = lax.fori_loop(1, NY, ey_add, ec[...])

    def g_out(k):
        return send(ef, eag.at[k], g_s.at[k], g_r.at[k], at_z(k))

    def g_out_start(k):
        g_out(k).start()

    loop(1, NZ, g_out_start)

    base = 6 * y
    for k in range(1, NY):
        y_copy(k).wait_recv()

    def z_copy(j):
        hold = 8 * (j // 3) + lax.rem(2 * x + c + HOLD[j % 3], 8)
        k = lax.rem(hold - z + NZ, NZ)
        return k, send(s2.at[j], rz.at[k], z_s.at[j], z_r.at[k], dev(x, y, hold, c))

    for j in range(6):
        s2[j] = (s1[base + j] + ry[1, j]) + (ry[2, j] + ry[3, j])
        k, copy = z_copy(j)

        @pl.when(k != 0)
        def _(copy=copy):
            copy.start()

    def n_add(k, total):
        n_copy(k).wait_recv()
        return total + rn[k]

    tr_o[...] = lax.fori_loop(1, NZ, n_add, nz[z])
    loop(1, NX, lambda k: g_copy(k).wait_recv())

    def tile_put(k):
        tile_o[lax.rem(x - k + NX, NX)] = rt[k]

    loop(1, NX, tile_put)
    tile_o[x] = gw[:, pl.ds(pl.multiple_of(x * 512, 512), 512)]

    loop(1, NZ, lambda k: g_out(k).wait_recv())

    def e_put(k):
        e_o[lax.rem(z - k + NZ, NZ)] = eag[k]

    loop(1, NZ, e_put)
    e_o[z] = ef[...]

    r = lax.rem(lax.rem(z, 8) - 2 * x - c + 16, 8)
    own_o[...] = s2[0]
    for p in range(3):

        @pl.when(r == HOLD[p])
        def _(p=p):
            def z_add(k, total):
                send(s2.at[0], rz.at[k], z_s.at[0], z_r.at[k], other).wait_recv()
                return total + rz[k]

            own_o[...] = lax.fori_loop(1, NZ, z_add, s2[3 * h + p])

    e_core.wait_send()
    m_core.wait_send()
    for i in range(4):
        core_chunk(i).wait_send()
    loop(1, NX, lambda k: g_copy(k).wait_send())
    loop(1, NZ, lambda k: e_copy(k).wait_send())
    loop(1, 16, lambda k: m_copy(k).wait_send())
    loop(1, NY, lambda k: y_copy(k).wait_send())
    loop(1, NY, lambda k: ey_copy(k).wait_send())
    loop(1, NZ, lambda k: n_copy(k).wait_send())
    loop(1, NZ, lambda k: g_out(k).wait_send())
    for j in range(6):
        k, copy = z_copy(j)

        @pl.when(k != 0)
        def _(copy=copy):
            copy.wait_send()


def trace_sums(tr):
    return jnp.sum(tr, axis=1, keepdims=True)


def inverse_kernel(own, e, tr, inv_own, inv_e):
    x, y, z, c = coords()
    sums = trace_sums(tr[...])
    low = z < 8
    ta = jnp.where(low, sums[1:2], sums[2:3])
    tg = jnp.where(low, sums[3:4], sums[4:5])
    ratio = jnp.sqrt((ta / (TOKENS * INNER)) / (tg / (TOKENS * WIDTH)))
    ratio_e = jnp.sqrt((TOKENS / VOCAB) / (sums[5:6] / (TOKENS * WIDTH)))
    is_g = lax.rem(lax.rem(z, 8) - 2 * x - c + 16, 8) == HOLD[2]
    shift = jnp.where(is_g, DAMP / ratio, DAMP * ratio)
    side = 2 * HEAD
    row = lax.broadcasted_iota(jnp.int32, (side, side), 0)
    lane = lax.broadcasted_iota(jnp.int32, (side, side), 1)
    eye = (row == lane).astype(F32)
    top = lax.broadcasted_iota(jnp.int32, (side, 1), 0) < HEAD

    def start(pair, amount):
        mat = blockdiag(pair) * (1.0 / TOKENS) + amount * eye
        sums = jnp.sum(jnp.abs(mat), axis=1, keepdims=True)
        bound = jnp.where(
            top,
            jnp.max(jnp.where(top, sums, 0.0), axis=0, keepdims=True),
            jnp.max(jnp.where(top, 0.0, sums), axis=0, keepdims=True),
        )
        return mat, eye / bound

    def fold(mat):
        return mat[:HEAD] + mat[HEAD:]

    m1, a1 = start(own[...], shift)
    m2, a2 = start(e[...], DAMP / ratio_e)
    for _ in range(NS_ITERS):
        i1 = jnp.dot(m1, a1, precision=HI, preferred_element_type=F32)
        i2 = jnp.dot(m2, a2, precision=HI, preferred_element_type=F32)
        a1 = jnp.dot(a1, 2.0 * eye - i1, precision=HI, preferred_element_type=F32)
        a2 = jnp.dot(a2, 2.0 * eye - i2, precision=HI, preferred_element_type=F32)
    inv_own[...] = fold(a1)
    inv_e[...] = fold(a2)


def spread_kernel(io, ie, a_o, g_o, e_o, ra, rg, re, a_s, a_r, g_s, g_r, e_s, e_r):
    x, y, z, c = coords()
    h = lax.div(z, 8)
    z8 = lax.rem(z, 8)
    u = 2 * x + c
    w = 2 * z8 + c

    def plane(k):
        v = lax.rem(u + k, 8)
        return dev(lax.div(v, 2), y, z, lax.rem(v, 2))

    def group(k):
        v = lax.rem(w + k, 16)
        return dev(x, y, 8 * h + lax.div(v, 2), lax.rem(v, 2))

    barrier = pltpu.get_barrier_semaphore()

    def greet_x(k):
        xx = lax.rem(x + 1 + lax.div(k, 2), NX)
        pl.semaphore_signal(barrier, inc=1, device_id=dev(xx, y, z, lax.rem(k, 2)), device_id_type=MESH)

    def greet_group(k):
        pl.semaphore_signal(barrier, inc=1, device_id=group(k), device_id_type=MESH)

    loop(0, 6, greet_x)
    loop(1, 16, greet_group)
    pl.semaphore_wait(barrier, 21)

    r = lax.rem(z8 - u + 16, 8)

    def a_copy(k, q):
        return send(io, ra.at[q], a_s.at[k], a_r.at[q], group(k))

    def g_copy(k):
        return send(io, rg, g_s.at[k], g_r, plane(k))

    def e_copy(k):
        return send(ie, re.at[k], e_s.at[k], e_r.at[k], plane(k))

    for p in range(2):

        @pl.when(r == HOLD[p])
        def _(p=p):
            loop(1, 16, lambda k: a_copy(k, 2 * c + p).start())

    @pl.when(r == HOLD[2])
    def _():
        loop(1, 8, lambda k: g_copy(k).start())

    loop(1, 8, lambda k: e_copy(k).start())

    e_o[u] = ie[...]

    def e_take(k):
        e_copy(k).wait_recv()
        e_o[lax.rem(u - k + 8, 8)] = re[k]

    loop(1, 8, e_take)

    @pl.when(r != HOLD[2])
    def _():
        g_copy(1).wait_recv()
        g_o[...] = rg[...]

    @pl.when(r == HOLD[2])
    def _():
        g_o[...] = io[...]

    for q in range(4):
        mine = (c == q // 2) & (r == HOLD[q % 2])

        @pl.when(mine)
        def _(q=q):
            a_o[q] = io[...]

        @pl.when(jnp.logical_not(mine))
        def _(q=q):
            a_copy(1, q).wait_recv()
            a_o[q] = ra[q]

    for p in range(2):

        @pl.when(r == HOLD[p])
        def _(p=p):
            loop(1, 16, lambda k: a_copy(k, 2 * c + p).wait_send())

    @pl.when(r == HOLD[2])
    def _():
        loop(1, 8, lambda k: g_copy(k).wait_send())

    loop(1, 8, lambda k: e_copy(k).wait_send())


def update_kernel(a, g, e, tile, ge, tr, w_o, e_o):
    x, y, z, c = coords()
    pair = g[...]
    g_block = jnp.where(c == 0, pair[:, :HEAD], pair[:, HEAD:])
    left = jnp.dot(g_block, tile[...], precision=HI, preferred_element_type=F32)
    for q in range(4):
        cols = slice(128 * q, 128 * q + 128)
        w_o[:, cols] = jnp.dot(left[:, cols], blockdiag(a[q]), precision=HI, preferred_element_type=F32)
    stats = tr[...]
    sums = trace_sums(stats)
    ratio_e = jnp.sqrt((TOKENS / VOCAB) / (sums[5:6] / (TOKENS * WIDTH)))
    lane = lax.broadcasted_iota(jnp.int32, (16, 128), 1)
    row = lax.broadcasted_iota(jnp.int32, (16, 128), 0)
    picked = jnp.where(lane == row + (64 * c + 16 * x), jnp.broadcast_to(stats[0:1], (16, 128)), 0.0)
    row_scale = jnp.sum(picked, axis=1, keepdims=True) + DAMP * ratio_e
    for u in range(8):
        cols = slice(128 * u, 128 * u + 128)
        e_o[:, cols] = jnp.dot(ge[:, cols], blockdiag(e[u]), precision=HI, preferred_element_type=F32) / row_scale


def vmem(count):
    return [pl.BlockSpec(memory_space=pltpu.VMEM)] * count


def shape(*dims):
    return jax.ShapeDtypeStruct(dims, F32)


def local(acts, out_cot, emb_ids, emb_cot, grad_w, grad_e):
    blk, eblk, m = pl.pallas_call(
        gram_kernel,
        out_shape=(shape(2, 24, 64, 128), shape(2, 64, 128), shape(4, 24, 128)),
        in_specs=vmem(5),
        out_specs=tuple(vmem(3)),
        name="grams",
    )(acts, out_cot, emb_cot, emb_ids.reshape(1, 64), emb_ids.reshape(64, 1))
    dma = pltpu.SemaphoreType.DMA
    own, e, tr, tile = pl.pallas_call(
        reduce_kernel,
        out_shape=(shape(64, 128), shape(16, 4, 128), shape(8, 128), shape(4, 16, 512)),
        in_specs=vmem(4),
        out_specs=tuple(vmem(4)),
        scratch_shapes=[
            pltpu.VMEM((24, 64, 128), F32),
            pltpu.VMEM((64, 128), F32),
            pltpu.VMEM((4, 24, 128), F32),
            pltpu.VMEM((24, 64, 128), F32),
            pltpu.VMEM((16, 4, 128), F32),
            pltpu.VMEM((4, 24, 128), F32),
            pltpu.VMEM((16, 8, 128), F32),
            pltpu.VMEM((4, 128), F32),
            pltpu.VMEM((4, 128), F32),
            pltpu.VMEM((6, 64, 128), F32),
            pltpu.VMEM((4, 6, 64, 128), F32),
            pltpu.VMEM((16, 4, 128), F32),
            pltpu.VMEM((16, 24, 128), F32),
            pltpu.VMEM((4, 4, 128), F32),
            pltpu.VMEM((16, 64, 128), F32),
            pltpu.VMEM((16, 8, 128), F32),
            pltpu.VMEM((16, 4, 128), F32),
            pltpu.VMEM((4, 16, 512), F32),
        ]
        + [dma((n,)) for n in (6, 6, 4, 4, 16, 16, 16, 16, 4, 4, 6, 16, 16, 16, 16, 16, 4, 4)],
        compiler_params=pltpu.CompilerParams(collective_id=0, has_side_effects=True),
        name="reduce",
    )(blk, eblk, m, grad_w)
    inv_own, inv_e = pl.pallas_call(
        inverse_kernel,
        out_shape=(shape(64, 128), shape(64, 128)),
        in_specs=vmem(3),
        out_specs=tuple(vmem(2)),
        name="inverse",
    )(own, e.reshape(64, 128), tr)
    inv_a, inv_g, all_e = pl.pallas_call(
        spread_kernel,
        out_shape=(shape(4, 64, 128), shape(64, 128), shape(8, 64, 128)),
        in_specs=vmem(2),
        out_specs=tuple(vmem(3)),
        scratch_shapes=[
            pltpu.VMEM((4, 64, 128), F32),
            pltpu.VMEM((64, 128), F32),
            pltpu.VMEM((8, 64, 128), F32),
            dma((16,)), dma((4,)), dma((8,)), dma, dma((8,)), dma((8,)),
        ],
        compiler_params=pltpu.CompilerParams(collective_id=1, has_side_effects=True),
        name="spread",
    )(inv_own, inv_e)
    return pl.pallas_call(
        update_kernel,
        out_shape=(shape(64, 512), shape(16, 1024)),
        in_specs=vmem(6),
        out_specs=tuple(vmem(2)),
        name="update",
    )(inv_a, inv_g, all_e, tile.reshape(64, 512), grad_e, tr)


def solution(mesh):
    in_specs = (
        P(None, "dp", "tensor"),
        P(None, "dp", "tensor"),
        P(("dp", "tensor")),
        P("dp", "tensor"),
        P(("dp", "tensor"), None),
        P(("dp", "tensor"), None),
    )
    out_specs = (P("dp", "tensor"), P(("dp", "tensor"), None))
    return jax.shard_map(local, mesh=mesh, in_specs=in_specs, out_specs=out_specs, check_vma=False)
```

time: 589 us -> 79 us (0.13)
  waiting for transfers between devices: 406 us -> 0 us
  blocking collectives: 112 us -> 0 us
  Pallas kernels: 0 us -> 76.4 us
  local copies, waits for them, and re-layouts: 30.4 us -> 1.35 us
  between operations: 15.5 us -> 0.65 us
  other arithmetic: 11 us -> 0 us
  matrix products: 10.1 us -> 0 us
    unnamed x4 -> x0, waiting for transfers between devices: 237 us -> none
    all_gather x2 -> x0, waiting for transfers between devices: 164 us -> none  [the longest x1 140 us: local(): lax.all_gather(inverse_mine.reshape(owned, HEAD * HEAD), 'dp', axis=0, ti...]
    psum x1 -> x0, blocking collectives: 112 us -> none  [local(): traces, counts_all = lax.psum((trace_local, local_counts), ('dp', 'tensor'))]
    pallas_call x0 -> x5, Pallas kernels: none -> 76.4 us  [the longest x1 44.2 us: local(): pl.pallas_call(reduce_kernel, out_shape=(shape(64, 128), shape(16, 4, 128...]
    unnamed x20 -> x0, local copies, waits for them, and re-layouts: 10.6 us -> none
    dot_general x14 -> x0, matrix products: 10.1 us -> none  [the longest x1 3 us: local(): jnp.einsum('lthi,lthj->lhij', split_acts, split_acts, preferred_element_t...]
    slice x6 -> x0, local copies, waits for them, and re-layouts: 6 us -> none  [the longest x1 2.68 us: local(): inverses[:layers * heads_part].reshape(layers, heads_part, HEAD, HEAD)]
  transfers between devices with their start and end apart: 4 -> 0, of which waited for: 4 -> 0; matrix products, arithmetic and copies ran while one was open for 2% -> 0% of each run, Pallas kernels for 0% -> 0%
where the time goes in v1:
time: 79 us; the launch traced here: 78.4 us
  Pallas kernels  76.4 us (97%)
  local copies, waits for them, and re-layouts  1.35 us (2%)
    pallas_call x1, Pallas kernels, local(): pl.pallas_call(reduce_kernel, out_shape=(shape(64, 128), shape(16, 4, 128...  44.2 us
    pallas_call x1, Pallas kernels, local(): pl.pallas_call(spread_kernel, out_shape=(shape(4, 64, 128), shape(64, 128...  21.7 us
    pallas_call x1, Pallas kernels, local(): pl.pallas_call(gram_kernel, out_shape=(shape(2, 24, 64, 128), shape(2, 64...  4.2 us
    pallas_call x1, Pallas kernels, local(): pl.pallas_call(inverse_kernel, out_shape=(shape(64, 128), shape(64, 128))...  3.62 us
    pallas_call x1, Pallas kernels, local(): pl.pallas_call(update_kernel, out_shape=(shape(64, 512), shape(16, 1024))...  2.77 us

profile of v1, /device:TPU:1, one launch (start us, length us, event | category | flops | bytes accessed | tf_op | source)
XLA Modules:
  0.0 78.4 jit_solution(12205819770370332258)
XLA Ops:
  0.6 1.3 %copy.8.ids_col = s32[64,1]{1,0:T(8,128)} copy(s32[64,1]{0,1:T(1,128)} %bitcast.6) | data formatting | bytes 512 | tf_op jit(solution)/shard_map/reshape | solution.py:484
  2.0 4.2 %grams.1 = (f32[2,24,64,128]{3,2,1,0:T(8,128)}, f32[2,64,128]{2,1,0:T(8,128)}, f32[4,24,128]{2,1,0:T(8,128)}) custom-call(bf16[8,256,512]{2,1,0:T(8,128)(2,1)} %acts.1, bf16[8,256,256]{2,1,0:T(8,128)(2,1)} %cot.1, bf16[256,256]{1,0:T(8,128)(2,1)} %emb.1, s32[1,64]{1,0:T(1,128)} %bitcast.7, s32[64,1]{1,0:T(8,128)} %copy.8.ids_col), custom_call_target="tpu_custom_call" | custom-call | tf_op jit(solution)/shard_map/grams/pallas_call | solution.py:478
  6.2 44.2 %reduce.1 = (f32[64,128]{1,0:T(8,128)}, f32[16,4,128]{2,1,0:T(4,128)}, f32[8,128]{1,0:T(8,128)}, f32[4,16,512]{2,1,0:T(8,128)}) custom-call(f32[2,24,64,128]{3,2,1,0:T(8,128)} %get-tuple-element.14.blk, f32[2,64,128]{2,1,0:T(8,128)} %get-tuple-element.15.eblk, f32[4,24,128]{2,1,0:T(8,128)} %get-tuple-element.16.m, f32[16,2048]{1,0:T(8,128)} %gw.1), custom_call_target="tpu_custom_call" | custom-call | tf_op jit(solution)/shard_map/reduce/pallas_call | solution.py:486
  50.3 3.6 %inverse.1 = (f32[64,128]{1,0:T(8,128)}, f32[64,128]{1,0:T(8,128)}) custom-call(f32[64,128]{1,0:T(8,128)} %get-tuple-element.17.own, f32[64,128]{1,0:T(8,128)} %bitcast.5, f32[8,128]{1,0:T(8,128)} %get-tuple-element.19.tr), custom_call_target="tpu_custom_call" | custom-call | tf_op jit(solution)/shard_map/inverse/pallas_call | solution.py:515
  54.0 21.7 %spread.1 = (f32[4,64,128]{2,1,0:T(8,128)}, f32[64,128]{1,0:T(8,128)}, f32[8,64,128]{2,1,0:T(8,128)}) custom-call(f32[64,128]{1,0:T(8,128)} %get-tuple-element.20.io, f32[64,128]{1,0:T(8,128)} %get-tuple-element.21.ie), custom_call_target="tpu_custom_call" | custom-call | tf_op jit(solution)/shard_map/spread/pallas_call | solution.py:522
  75.6 2.8 %update.1 = (f32[64,512]{1,0:T(8,128)}, f32[16,1024]{1,0:T(8,128)}) custom-call(f32[4,64,128]{2,1,0:T(8,128)} %get-tuple-element.22.a, f32[64,128]{1,0:T(8,128)} %get-tuple-element.23.g, f32[8,64,128]{2,1,0:T(8,128)} %get-tuple-element.24.e, f32[64,512]{1,0:T(8,128)} %bitcast.4, f32[16,1024]{1,0:T(8,128)} %ge.1, f32[8,128]{1,0:T(8,128)} %get-tuple-element.19.tr), custom_call_target="tpu_custom_call" | custom-call | tf_op jit(solution)/shard_map/update/pallas_call | solution.py:536

commit v2 on v1

v2 whole, which is shorter than its diff:
```python
import jax
import jax.numpy as jnp
from jax import lax
from jax.experimental import pallas as pl
from jax.experimental.pallas import tpu as pltpu
from jax.sharding import PartitionSpec as P

HEAD = 64
NS_ITERS = 4
DAMP = 0.7
LAYERS = 8
TOKENS = 32768
VOCAB = 8192
WIDTH = 1024
INNER = 2048
NX, NY, NZ = 4, 4, 16
MESH = pl.DeviceIdType.MESH
F32 = jnp.float32
HI = lax.Precision.HIGHEST


def coords():
    d = lax.axis_index("dp").astype(jnp.int32)
    x = lax.axis_index("tensor").astype(jnp.int32)
    c = lax.rem(d, 2)
    z = lax.rem(lax.div(d, 2), NZ)
    y = lax.div(d, 2 * NZ)
    return x, y, z, c


def dev(x, y, z, c):
    return ((y * NZ + z) * 2 + c, x)


def hold(x, c, p):
    u = 2 * x + c
    if p == 2:
        return u
    if p == 0:
        return 3 - c
    return jnp.where(c == 0, jnp.where(u == 4, 5, 4), jnp.where(u == 5, 4, 5))


def send(src, dst, send_sem, recv_sem, device):
    return pltpu.make_async_remote_copy(
        src_ref=src, dst_ref=dst, send_sem=send_sem, recv_sem=recv_sem, device_id=device, device_id_type=MESH
    )


def loop(low, high, body):
    def step(k, carry):
        body(k)
        return carry

    lax.fori_loop(low, high, step, 0)


def pair_of(product):
    lane = lax.broadcasted_iota(jnp.int32, (HEAD, 2 * HEAD), 1)
    return jnp.where(lane < HEAD, product[:HEAD], product[HEAD:])


def blockdiag(pair):
    lane = lax.broadcasted_iota(jnp.int32, (HEAD, 2 * HEAD), 1)
    zero = jnp.zeros_like(pair)
    return jnp.concatenate([jnp.where(lane < HEAD, pair, zero), jnp.where(lane < HEAD, zero, pair)], axis=0)


def grams(acts, cot, emb, ids_row, blk, eblk, m):
    lane = lax.broadcasted_iota(jnp.int32, (HEAD, 2 * HEAD), 1)
    row = lax.broadcasted_iota(jnp.int32, (HEAD, 2 * HEAD), 0)
    on_diag = (lane == row) | (lane == row + HEAD)

    def gram(x):
        full = lax.dot_general(x, x, (((0,), (0,)), ((), ())), preferred_element_type=F32)
        pair = pair_of(full)
        return pair, jnp.sum(jnp.where(on_diag, pair, 0.0), axis=0, keepdims=True)

    ids = ids_row[...]
    hit_row = (lax.broadcasted_iota(jnp.int32, (64, 64), 0) == lax.shift_right_logical(ids, 7)).astype(F32)
    hit_lane = (lax.broadcasted_iota(jnp.int32, (128, 64), 0) == (ids & 127)).astype(F32)
    hist = lax.dot_general(
        hit_row.astype(jnp.bfloat16),
        hit_lane.astype(jnp.bfloat16),
        (((1,), (1,)), ((), ())),
        preferred_element_type=F32,
    )
    sum_e = jnp.zeros((1, 128), F32)
    for core in range(2):
        pair, diag = gram(emb[:, 128 * core : 128 * core + 128])
        eblk[core] = pair
        sum_e = sum_e + diag
    rows = {}
    for layer in range(LAYERS):
        sum_a = jnp.zeros((1, 128), F32)
        sum_g = jnp.zeros((1, 128), F32)
        for core in range(2):
            for p in range(2):
                q = 2 * core + p
                pair, diag = gram(acts[layer, :, 128 * q : 128 * q + 128])
                blk[core, 3 * layer + p] = pair
                sum_a = sum_a + diag
            pair, diag = gram(cot[layer, :, 128 * core : 128 * core + 128])
            blk[core, 3 * layer + 2] = pair
            sum_g = sum_g + diag
        rows[layer] = (sum_a, sum_g)
    for y in range(NY):
        m[y, 0:16] = hist[16 * y : 16 * y + 16]
        tail = [rows[2 * y][0], rows[2 * y + 1][0], rows[2 * y][1], rows[2 * y + 1][1], sum_e]
        m[y, 16:24] = jnp.concatenate(tail + [jnp.zeros((3, 128), F32)], axis=0)


def trace_sums(tr):
    return jnp.sum(tr, axis=1, keepdims=True)


def inverses(own, e, tr):
    x, y, z, c = coords()
    sums = trace_sums(tr)
    low = z < 8
    ta = jnp.where(low, sums[1:2], sums[2:3])
    tg = jnp.where(low, sums[3:4], sums[4:5])
    ratio = jnp.sqrt((ta / (TOKENS * INNER)) / (tg / (TOKENS * WIDTH)))
    ratio_e = jnp.sqrt((TOKENS / VOCAB) / (sums[5:6] / (TOKENS * WIDTH)))
    is_g = lax.rem(z, 8) == hold(x, c, 2)
    shift = jnp.where(is_g, DAMP / ratio, DAMP * ratio)
    side = 2 * HEAD
    row = lax.broadcasted_iota(jnp.int32, (side, side), 0)
    lane = lax.broadcasted_iota(jnp.int32, (side, side), 1)
    eye = (row == lane).astype(F32)
    top = lax.broadcasted_iota(jnp.int32, (side, 1), 0) < HEAD

    def start(pair, amount):
        mat = blockdiag(pair) * (1.0 / TOKENS) + amount * eye
        sums = jnp.sum(jnp.abs(mat), axis=1, keepdims=True)
        bound = jnp.where(
            top,
            jnp.max(jnp.where(top, sums, 0.0), axis=0, keepdims=True),
            jnp.max(jnp.where(top, 0.0, sums), axis=0, keepdims=True),
        )
        return mat, eye / bound

    def fold(mat):
        return mat[:HEAD] + mat[HEAD:]

    m1, a1 = start(own, shift)
    m2, a2 = start(e, DAMP / ratio_e)
    for _ in range(NS_ITERS):
        i1 = jnp.dot(m1, a1, precision=HI, preferred_element_type=F32)
        i2 = jnp.dot(m2, a2, precision=HI, preferred_element_type=F32)
        a1 = jnp.dot(a1, 2.0 * eye - i1, precision=HI, preferred_element_type=F32)
        a2 = jnp.dot(a2, 2.0 * eye - i2, precision=HI, preferred_element_type=F32)
    return fold(a1), fold(a2)


def whole_kernel(
    acts, cot, emb, ids_row, gw, ge, w_o, u_o,
    blk, eblk, m, own_v, e_v, tr_v,
    rblk, reb, rm, s1, se, ms, nz, ec, ef, s2, ry, re, rmm, rey, rz, rn, eag, rt,
    io, ie, ra, rg, ree,
    c_s, c_r, y_s, y_r, e_s, e_r, m_s, m_r, ey_s, ey_r, z_s, z_r, n_s, n_r, g_s, g_r, t_s, t_r,
    a_s, a_r, f_s, ig_s, ig_r, ie_s, ie_r,
):
    x, y, z, c = coords()
    h = lax.div(z, 8)
    z8 = lax.rem(z, 8)
    u = 2 * x + c
    other = dev(x, y, z, 1 - c)

    def at_xy(k):
        return lax.rem(x + lax.div(k, 4), 4), lax.rem(y + lax.rem(k, 4), 4)

    def at_z(k):
        return dev(x, y, lax.rem(z + k, NZ), c)

    def at_y(k):
        return dev(x, lax.rem(y + k, NY), z, c)

    def at_x(k):
        return dev(lax.rem(x + k, NX), y, z, c)

    barrier = pltpu.get_barrier_semaphore()
    pl.semaphore_signal(barrier, inc=1, device_id=other, device_id_type=MESH)

    def greet_xy(k):
        xx, yy = at_xy(k)
        pl.semaphore_signal(barrier, inc=1, device_id=dev(xx, yy, z, c), device_id_type=MESH)

    def greet_z(k):
        pl.semaphore_signal(barrier, inc=1, device_id=at_z(k), device_id_type=MESH)

    def greet_group(k):
        near = 8 * h + lax.rem(z8 + k, 8)
        pl.semaphore_signal(barrier, inc=1, device_id=dev(x, y, near, 1 - c), device_id_type=MESH)

    def greet_plane(k):
        pl.semaphore_signal(barrier, inc=1, device_id=dev(lax.rem(x + k, NX), y, z, 1 - c), device_id_type=MESH)

    loop(1, 16, greet_xy)
    loop(1, 16, greet_z)
    loop(1, 8, greet_group)
    loop(1, NX, greet_plane)
    grams(acts, cot, emb, ids_row, blk, eblk, m)
    pl.semaphore_wait(barrier, 41)

    def core_chunk(i):
        k = (2, 1, 3, 0)[i]
        yy = lax.rem(y + k, NY)
        part = pl.ds(6 * yy, 6)
        return send(blk.at[1 - c, part], rblk.at[part], c_s.at[i], c_r.at[i], other)

    e_core = send(eblk.at[1 - c], reb, c_s.at[4], c_r.at[4], other)
    m_core = send(m, rm, c_s.at[5], c_r.at[5], other)
    e_core.start()
    m_core.start()
    for i in range(4):
        core_chunk(i).start()

    def g_copy(k):
        cols = pl.ds(pl.multiple_of(lax.rem(x + k, NX) * 512, 512), 512)
        return send(gw.at[:, cols], rt.at[x], t_s.at[k], t_r.at[k], at_x(k))

    def g_start(k):
        g_copy(k).start()

    loop(1, NX, g_start)

    e_core.wait_recv()
    e_sum = eblk[c] + reb[...]
    for k in range(NZ):
        se[k] = e_sum[4 * k : 4 * k + 4]

    def e_copy(k):
        return send(se.at[lax.rem(z + k, NZ)], re.at[k], e_s.at[k], e_r.at[k], at_z(k))

    def e_start(k):
        e_copy(k).start()

    loop(1, NZ, e_start)
    m_core.wait_recv()
    for k in range(NY):
        ms[k] = m[k] + rm[k]

    def m_copy(k):
        xx, yy = at_xy(k)
        return send(ms.at[yy], rmm.at[k], m_s.at[k], m_r.at[k], dev(xx, yy, z, c))

    def m_start(k):
        m_copy(k).start()

    loop(1, 16, m_start)

    def y_copy(k):
        part = pl.ds(6 * lax.rem(y + k, NY), 6)
        return send(s1.at[part], ry.at[k], y_s.at[k], y_r.at[k], at_y(k))

    for i in range(4):
        k = (2, 1, 3, 0)[i]
        core_chunk(i).wait_recv()
        first = 6 * lax.rem(y + k, NY)

        def add(j, first=first):
            s1[first + j] = blk[c, first + j] + rblk[first + j]

        loop(0, 6, add)
        if k:
            y_copy(k).start()

    def e_add(k, total):
        e_copy(k).wait_recv()
        return total + re[k]

    ec[...] = lax.fori_loop(1, NZ, e_add, se[z])

    def ey_copy(k):
        return send(ec, rey.at[k], ey_s.at[k], ey_r.at[k], at_y(k))

    def ey_start(k):
        ey_copy(k).start()

    loop(1, NY, ey_start)

    def m_add(k, total):
        m_copy(k).wait_recv()
        return total + rmm[k]

    n = lax.fori_loop(1, 16, m_add, ms[y])
    for k in range(NZ):
        nz[k] = jnp.concatenate([n[k : k + 1], n[16:23]], axis=0)

    def n_copy(k):
        return send(nz.at[lax.rem(z + k, NZ)], rn.at[k], n_s.at[k], n_r.at[k], at_z(k))

    def n_start(k):
        n_copy(k).start()

    loop(1, NZ, n_start)

    def ey_add(k, total):
        ey_copy(k).wait_recv()
        return total + rey[k]

    ef[...] = lax.fori_loop(1, NY, ey_add, ec[...])

    def g_out(k):
        return send(ef, eag.at[z], g_s.at[k], g_r.at[k], at_z(k))

    def g_out_start(k):
        g_out(k).start()

    loop(1, NZ, g_out_start)

    base = 6 * y
    for k in range(1, NY):
        y_copy(k).wait_recv()

    def z_copy(j):
        place = 8 * (j // 3) + hold(x, c, j % 3)
        k = lax.rem(place - z + NZ, NZ)
        return k, send(s2.at[j], rz.at[k], z_s.at[j], z_r.at[k], dev(x, y, place, c))

    for j in range(6):
        s2[j] = (s1[base + j] + ry[1, j]) + (ry[2, j] + ry[3, j])
        k, copy = z_copy(j)

        @pl.when(k != 0)
        def _(copy=copy):
            copy.start()

    def n_add(k, total):
        n_copy(k).wait_recv()
        return total + rn[k]

    tr_v[...] = lax.fori_loop(1, NZ, n_add, nz[z])
    loop(1, NZ, lambda k: g_out(k).wait_recv())
    eag[z] = ef[...]
    for k in range(NZ):
        e_v[4 * k : 4 * k + 4] = eag[k]

    own_v[...] = s2[0]
    for p in range(3):

        @pl.when(z8 == hold(x, c, p))
        def _(p=p):
            def z_add(k, total):
                send(s2.at[0], rz.at[k], z_s.at[0], z_r.at[k], other).wait_recv()
                return total + rz[k]

            own_v[...] = lax.fori_loop(1, NZ, z_add, s2[3 * h + p])

    inv_own, inv_e = inverses(own_v[...], e_v[...], tr_v[...])
    io[...] = inv_own
    ie[...] = inv_e

    def a_copy(k, q):
        near = 8 * h + lax.rem(z8 + k, 8)
        return send(io, ra.at[q], a_s.at[k], a_r.at[q], dev(x, y, near, lax.rem(q, 2)))

    def a_side(q):
        return send(io, ra.at[q], a_s.at[0], a_r.at[q], other)

    def a_pass(q):
        return send(ra.at[q], ra.at[q], f_s.at[q], a_r.at[q], other)

    def plane(k):
        v = lax.rem(u + k, 8)
        return dev(lax.div(v, 2), y, z, lax.rem(v, 2))

    def ig_copy(k):
        return send(io, rg, ig_s.at[k], ig_r, plane(k))

    def ie_copy(k):
        return send(ie, ree.at[u], ie_s.at[k], ie_r.at[k], plane(k))

    for p in range(2):

        @pl.when(z8 == hold(x, c, p))
        def _(p=p):
            loop(1, 8, lambda k: a_copy(k, 2 * c + p).start())
            a_side(2 * c + p).start()
            ra[2 * c + p] = inv_own

    @pl.when(z8 == hold(x, c, 2))
    def _():
        loop(1, 8, lambda k: ig_copy(k).start())
        rg[...] = inv_own

    loop(1, 8, lambda k: ie_copy(k).start())
    ree[u] = inv_e
    loop(1, NX, lambda k: g_copy(k).wait_recv())
    rt[x] = gw[:, pl.ds(pl.multiple_of(x * 512, 512), 512)]

    @pl.when(z8 != hold(x, c, 2))
    def _():
        ig_copy(1).wait_recv()

    pair = rg[...]
    g_block = jnp.where(c == 0, pair[:, :HEAD], pair[:, HEAD:])
    tile = jnp.concatenate([rt[k] for k in range(NX)], axis=0)
    left = jnp.dot(g_block, tile, precision=HI, preferred_element_type=F32)
    for q in range(4):
        here = z8 == hold(x, q // 2, q % 2)

        @pl.when(jnp.logical_not(here) & (c == q % 2))
        def _(q=q):
            a_side(q).wait_recv()
            a_pass(q).start()

    loop(1, 8, lambda k: ie_copy(k).wait_recv())
    stats = tr_v[...]
    ratio_e = jnp.sqrt((TOKENS / VOCAB) / (trace_sums(stats)[5:6] / (TOKENS * WIDTH)))
    lane = lax.broadcasted_iota(jnp.int32, (16, 128), 1)
    row = lax.broadcasted_iota(jnp.int32, (16, 128), 0)
    picked = jnp.where(lane == row + (64 * c + 16 * x), jnp.broadcast_to(stats[0:1], (16, 128)), 0.0)
    row_scale = jnp.sum(picked, axis=1, keepdims=True) + DAMP * ratio_e
    for v in range(8):
        cols = slice(128 * v, 128 * v + 128)
        u_o[:, cols] = jnp.dot(ge[:, cols], blockdiag(ree[v]), precision=HI, preferred_element_type=F32) / row_scale
    for q in range(4):
        here = z8 == hold(x, q // 2, q % 2)

        @pl.when((here & (c != q // 2)) | (jnp.logical_not(here) & (c != q % 2)))
        def _(q=q):
            a_side(q).wait_recv()

        cols = slice(128 * q, 128 * q + 128)
        w_o[:, cols] = jnp.dot(left[:, cols], blockdiag(ra[q]), precision=HI, preferred_element_type=F32)

    for p in range(2):

        @pl.when(z8 == hold(x, c, p))
        def _(p=p):
            loop(1, 8, lambda k: a_copy(k, 2 * c + p).wait_send())
            a_side(2 * c + p).wait_send()

    for q in range(4):
        here = z8 == hold(x, q // 2, q % 2)

        @pl.when(jnp.logical_not(here) & (c == q % 2))
        def _(q=q):
            a_pass(q).wait_send()

    @pl.when(z8 == hold(x, c, 2))
    def _():
        loop(1, 8, lambda k: ig_copy(k).wait_send())

    loop(1, 8, lambda k: ie_copy(k).wait_send())
    e_core.wait_send()
    m_core.wait_send()
    for i in range(4):
        core_chunk(i).wait_send()
    loop(1, NX, lambda k: g_copy(k).wait_send())
    loop(1, NZ, lambda k: e_copy(k).wait_send())
    loop(1, 16, lambda k: m_copy(k).wait_send())
    loop(1, NY, lambda k: y_copy(k).wait_send())
    loop(1, NY, lambda k: ey_copy(k).wait_send())
    loop(1, NZ, lambda k: n_copy(k).wait_send())
    loop(1, NZ, lambda k: g_out(k).wait_send())
    for j in range(6):
        k, copy = z_copy(j)

        @pl.when(k != 0)
        def _(copy=copy):
            copy.wait_send()


def vmem(count):
    return [pl.BlockSpec(memory_space=pltpu.VMEM)] * count


def shape(*dims):
    return jax.ShapeDtypeStruct(dims, F32)


def local(acts, out_cot, emb_ids, emb_cot, grad_w, grad_e):
    dma = pltpu.SemaphoreType.DMA
    buffers = [
        (2, 24, 64, 128), (2, 64, 128), (4, 24, 128), (64, 128), (64, 128), (8, 128),
        (24, 64, 128), (64, 128), (4, 24, 128), (24, 64, 128), (16, 4, 128), (4, 24, 128),
        (16, 8, 128), (4, 128), (4, 128), (6, 64, 128), (4, 6, 64, 128), (16, 4, 128),
        (16, 24, 128), (4, 4, 128), (16, 64, 128), (16, 8, 128), (16, 4, 128), (4, 16, 512),
        (64, 128), (64, 128), (4, 64, 128), (64, 128), (8, 64, 128),
    ]
    return pl.pallas_call(
        whole_kernel,
        out_shape=(shape(64, 512), shape(16, 1024)),
        in_specs=vmem(6),
        out_specs=tuple(vmem(2)),
        scratch_shapes=[pltpu.VMEM(dims, F32) for dims in buffers]
        + [dma((n,)) for n in (6, 6, 4, 4, 16, 16, 16, 16, 4, 4, 6, 16, 16, 16, 16, 16, 4, 4)]
        + [dma((8,)), dma((4,)), dma((4,)), dma((8,)), dma, dma((8,)), dma((8,))],
        compiler_params=pltpu.CompilerParams(collective_id=0, has_side_effects=True),
        name="whole",
    )(acts, out_cot, emb_cot, emb_ids.reshape(1, 64), grad_w, grad_e)


def solution(mesh):
    in_specs = (
        P(None, "dp", "tensor"),
        P(None, "dp", "tensor"),
        P(("dp", "tensor")),
        P("dp", "tensor"),
        P(("dp", "tensor"), None),
        P(("dp", "tensor"), None),
    )
    out_specs = (P("dp", "tensor"), P(("dp", "tensor"), None))
    return jax.shard_map(local, mesh=mesh, in_specs=in_specs, out_specs=out_specs, check_vma=False)
```

time: 79 us -> 66.5 us (0.84)
  Pallas kernels: 76.4 us -> 61.7 us
  local copies, waits for them, and re-layouts: 1.35 us -> 3.04 us
    pallas_call x5 -> x1, Pallas kernels: 76.4 us -> 61.7 us  [local(): pl.pallas_call(whole_kernel, out_shape=(shape(64, 512), shape(16, 1024)),...]
    unnamed x0 -> x2, local copies, waits for them, and re-layouts: none -> 3.04 us
    reshape x1 -> x0, local copies, waits for them, and re-layouts: 1.35 us -> none  [local(): emb_ids.reshape(64, 1)]
where the time goes in v2:
time: 66.5 us; the launch traced here: 65.4 us
  Pallas kernels  61.7 us (93%)
  local copies, waits for them, and re-layouts  3.04 us (5%)
    pallas_call x1, Pallas kernels, local(): pl.pallas_call(whole_kernel, out_shape=(shape(64, 512), shape(16, 1024)),...  61.7 us
    unnamed x2, local copies, waits for them, and re-layouts  3.04 us

profile of v2, /device:TPU:1, one launch (start us, length us, event | category | flops | bytes accessed | tf_op | source)
XLA Modules:
  0.0 65.4 jit_solution(14277591741252725176)
XLA Ops:
  0.6 61.7 %whole.1 = (f32[64,512]{1,0:T(8,128)}, f32[16,1024]{1,0:T(8,128)}) custom-call(bf16[8,256,512]{2,1,0:T(8,128)(2,1)} %acts.1, bf16[8,256,256]{2,1,0:T(8,128)(2,1)} %cot.1, bf16[256,256]{1,0:T(8,128)(2,1)} %emb.1, s32[1,64]{1,0:T(1,128)} %bitcast.1, f32[16,2048]{1,0:T(8,128)} %gw.1, f32[16,1024]{1,0:T(8,128)} %ge.1), custom_call_target="tpu_custom_call" | custom-call | tf_op jit(solution)/shard_map/whole/pallas_call | solution.py:484
  62.3 1.6 %copy.10 = f32[64,512]{1,0:T(8,128)} copy(f32[64,512]{1,0:T(8,128)} %get-tuple-element.4) | data formatting | bytes 262144
  63.9 1.5 %copy.11 = f32[16,1024]{1,0:T(8,128)} copy(f32[16,1024]{1,0:T(8,128)} %get-tuple-element.5) | data formatting | bytes 131072

commit v3 on v2

--- a/solution.py
+++ b/solution.py
@@ -32,13 +32,8 @@
     return ((y * NZ + z) * 2 + c, x)
 
 
-def hold(x, c, p):
-    u = 2 * x + c
-    if p == 2:
-        return u
-    if p == 0:
-        return 3 - c
-    return jnp.where(c == 0, jnp.where(u == 4, 5, 4), jnp.where(u == 5, 4, 5))
+def a_place(core):
+    return 3 + core
 
 
 def send(src, dst, send_sem, recv_sem, device):
@@ -91,19 +86,28 @@
         eblk[core] = pair
         sum_e = sum_e + diag
     rows = {}
+    upper = row <= jnp.where(lane < HEAD, lane, lane - HEAD)
+    below = {}
     for layer in range(LAYERS):
+        y, odd = layer // 2, layer % 2
         sum_a = jnp.zeros((1, 128), F32)
         sum_g = jnp.zeros((1, 128), F32)
         for core in range(2):
-            for p in range(2):
-                q = 2 * core + p
-                pair, diag = gram(acts[layer, :, 128 * q : 128 * q + 128])
-                blk[core, 3 * layer + p] = pair
-                sum_a = sum_a + diag
-            pair, diag = gram(cot[layer, :, 128 * core : 128 * core + 128])
-            blk[core, 3 * layer + 2] = pair
-            sum_g = sum_g + diag
+            first, diag_first = gram(acts[layer, :, 256 * core : 256 * core + 128])
+            second, diag_second = gram(acts[layer, :, 256 * core + 128 : 256 * core + 256])
+            blk[core, y, 64 * odd : 64 * odd + 64] = jnp.where(upper, first, second)
+            below[core, odd] = diag_second
+            sum_a = sum_a + (diag_first + diag_second)
+        first, diag_first = gram(cot[layer, :, 0:128])
+        second, diag_second = gram(cot[layer, :, 128:256])
+        blk[odd, y, 128:192] = jnp.where(upper, first, second)
+        below[odd, 2] = diag_second
+        sum_g = sum_g + (diag_first + diag_second)
         rows[layer] = (sum_a, sum_g)
+        if odd:
+            for core in range(2):
+                diags = [below[core, 0], below[core, 1], below[core, 2], jnp.zeros((5, 128), F32)]
+                blk[core, y, 192:200] = jnp.concatenate(diags, axis=0)
     for y in range(NY):
         m[y, 0:16] = hist[16 * y : 16 * y + 16]
         tail = [rows[2 * y][0], rows[2 * y + 1][0], rows[2 * y][1], rows[2 * y + 1][1], sum_e]
@@ -122,7 +126,7 @@
     tg = jnp.where(low, sums[3:4], sums[4:5])
     ratio = jnp.sqrt((ta / (TOKENS * INNER)) / (tg / (TOKENS * WIDTH)))
     ratio_e = jnp.sqrt((TOKENS / VOCAB) / (sums[5:6] / (TOKENS * WIDTH)))
-    is_g = lax.rem(z, 8) == hold(x, c, 2)
+    is_g = lax.rem(z, 8) == 2 * x + c
     shift = jnp.where(is_g, DAMP / ratio, DAMP * ratio)
     side = 2 * HEAD
     row = lax.broadcasted_iota(jnp.int32, (side, side), 0)
@@ -143,21 +147,31 @@
     def fold(mat):
         return mat[:HEAD] + mat[HEAD:]
 
-    m1, a1 = start(own, shift)
+    both = own[:HEAD]
+    turned = fold(blockdiag(both).T)
+    at = lax.broadcasted_iota(jnp.int32, (HEAD, side), 0)
+    to = lax.broadcasted_iota(jnp.int32, (HEAD, side), 1)
+    to = jnp.where(to < HEAD, to, to - HEAD)
+    first = jnp.where(at <= to, both, turned)
+    second = jnp.where(at > to, both, jnp.where(at == to, own[HEAD : HEAD + 1], turned))
+    m0, a0 = start(first, shift)
+    m1, a1 = start(second, shift)
     m2, a2 = start(e, DAMP / ratio_e)
     for _ in range(NS_ITERS):
+        i0 = jnp.dot(m0, a0, precision=HI, preferred_element_type=F32)
         i1 = jnp.dot(m1, a1, precision=HI, preferred_element_type=F32)
         i2 = jnp.dot(m2, a2, precision=HI, preferred_element_type=F32)
+        a0 = jnp.dot(a0, 2.0 * eye - i0, precision=HI, preferred_element_type=F32)
         a1 = jnp.dot(a1, 2.0 * eye - i1, precision=HI, preferred_element_type=F32)
         a2 = jnp.dot(a2, 2.0 * eye - i2, precision=HI, preferred_element_type=F32)
-    return fold(a1), fold(a2)
+    return fold(a0), fold(a1), fold(a2)
 
 
 def whole_kernel(
     acts, cot, emb, ids_row, gw, ge, w_o, u_o,
     blk, eblk, m, own_v, e_v, tr_v,
     rblk, reb, rm, s1, se, ms, nz, ec, ef, s2, ry, re, rmm, rey, rz, rn, eag, rt,
-    io, ie, ra, rg, ree,
+    ia, ib, ie, ra, rg, ree,
     c_s, c_r, y_s, y_r, e_s, e_r, m_s, m_r, ey_s, ey_r, z_s, z_r, n_s, n_r, g_s, g_r, t_s, t_r,
     a_s, a_r, f_s, ig_s, ig_r, ie_s, ie_r,
 ):
@@ -165,6 +179,9 @@
     h = lax.div(z, 8)
     z8 = lax.rem(z, 8)
     u = 2 * x + c
+    z_near = z + 1 - 2 * lax.rem(z, 2)
+    is_a = z8 == a_place(c)
+    is_g = (z8 == u) & (h == c)
     other = dev(x, y, z, 1 - c)
 
     def at_xy(k):
@@ -199,15 +216,19 @@
     loop(1, 16, greet_xy)
     loop(1, 16, greet_z)
     loop(1, 8, greet_group)
+    def greet_near(k):
+        xx = lax.rem(x + 1 + lax.div(k, 2), NX)
+        pl.semaphore_signal(barrier, inc=1, device_id=dev(xx, y, z_near, lax.rem(k, 2)), device_id_type=MESH)
+
     loop(1, NX, greet_plane)
+    loop(0, 6, greet_near)
     grams(acts, cot, emb, ids_row, blk, eblk, m)
-    pl.semaphore_wait(barrier, 41)
+    pl.semaphore_wait(barrier, 47)
 
     def core_chunk(i):
         k = (2, 1, 3, 0)[i]
         yy = lax.rem(y + k, NY)
-        part = pl.ds(6 * yy, 6)
-        return send(blk.at[1 - c, part], rblk.at[part], c_s.at[i], c_r.at[i], other)
+        return send(blk.at[1 - c, yy], rblk.at[yy], c_s.at[i], c_r.at[i], other)
 
     e_core = send(eblk.at[1 - c], reb, c_s.at[4], c_r.at[4], other)
     m_core = send(m, rm, c_s.at[5], c_r.at[5], other)
@@ -251,18 +272,13 @@
     loop(1, 16, m_start)
 
     def y_copy(k):
-        part = pl.ds(6 * lax.rem(y + k, NY), 6)
-        return send(s1.at[part], ry.at[k], y_s.at[k], y_r.at[k], at_y(k))
+        return send(s1.at[lax.rem(y + k, NY)], ry.at[k], y_s.at[k], y_r.at[k], at_y(k))
 
     for i in range(4):
         k = (2, 1, 3, 0)[i]
         core_chunk(i).wait_recv()
-        first = 6 * lax.rem(y + k, NY)
-
-        def add(j, first=first):
-            s1[first + j] = blk[c, first + j] + rblk[first + j]
-
-        loop(0, 6, add)
+        yy = lax.rem(y + k, NY)
+        s1[yy] = blk[c, yy] + rblk[yy]
         if k:
             y_copy(k).start()
 
@@ -310,17 +326,18 @@
 
     loop(1, NZ, g_out_start)
 
-    base = 6 * y
     for k in range(1, NY):
         y_copy(k).wait_recv()
 
     def z_copy(j):
-        place = 8 * (j // 3) + hold(x, c, j % 3)
+        place = 8 * c + u if j == 2 else 8 * j + a_place(c)
         k = lax.rem(place - z + NZ, NZ)
         return k, send(s2.at[j], rz.at[k], z_s.at[j], z_r.at[k], dev(x, y, place, c))
 
-    for j in range(6):
-        s2[j] = (s1[base + j] + ry[1, j]) + (ry[2, j] + ry[3, j])
+    chunk = (s1[y] + ry[1]) + (ry[2] + ry[3])
+    for j in range(3):
+        s2[j, 0:64] = chunk[64 * j : 64 * j + 64]
+        s2[j, 64:72] = jnp.broadcast_to(chunk[192 + j : 193 + j], (8, 128))
         k, copy = z_copy(j)
 
         @pl.when(k != 0)
@@ -338,26 +355,26 @@
         e_v[4 * k : 4 * k + 4] = eag[k]
 
     own_v[...] = s2[0]
-    for p in range(3):
-
-        @pl.when(z8 == hold(x, c, p))
-        def _(p=p):
-            def z_add(k, total):
-                send(s2.at[0], rz.at[k], z_s.at[0], z_r.at[k], other).wait_recv()
-                return total + rz[k]
-
-            own_v[...] = lax.fori_loop(1, NZ, z_add, s2[3 * h + p])
-
-    inv_own, inv_e = inverses(own_v[...], e_v[...], tr_v[...])
-    io[...] = inv_own
-    ie[...] = inv_e
-
-    def a_copy(k, q):
+
+    @pl.when(is_a | is_g)
+    def _():
+        def z_add(k, total):
+            send(s2.at[0], rz.at[k], z_s.at[0], z_r.at[k], other).wait_recv()
+            return total + rz[k]
+
+        own_v[...] = lax.fori_loop(1, NZ, z_add, s2[jnp.where(is_a, h, 2)])
+
+    ia[...], ib[...], ie[...] = inverses(own_v[...], e_v[...], tr_v[...])
+
+    def a_copy(k, p):
         near = 8 * h + lax.rem(z8 + k, 8)
-        return send(io, ra.at[q], a_s.at[k], a_r.at[q], dev(x, y, near, lax.rem(q, 2)))
-
-    def a_side(q):
-        return send(io, ra.at[q], a_s.at[0], a_r.at[q], other)
+        return send((ia, ib)[p], ra.at[2 * c + p], a_s.at[8 * p + k], a_r.at[2 * c + p], dev(x, y, near, p))
+
+    def a_side(p):
+        return send((ia, ib)[p], ra.at[2 * c + p], a_s.at[8 * p], a_r.at[2 * c + p], other)
+
+    def a_came(q):
+        send(ia, ra.at[q], a_s.at[0], a_r.at[q], other).wait_recv()
 
     def a_pass(q):
         return send(ra.at[q], ra.at[q], f_s.at[q], a_r.at[q], other)
@@ -366,44 +383,54 @@
         v = lax.rem(u + k, 8)
         return dev(lax.div(v, 2), y, z, lax.rem(v, 2))
 
-    def ig_copy(k):
-        return send(io, rg, ig_s.at[k], ig_r, plane(k))
+    def near_plane(k):
+        return dev(lax.div(k, 2), y, z_near, lax.rem(k, 2))
+
+    def ig_here(p, k):
+        return send((ia, ib)[p], rg, ig_s.at[k], ig_r, plane(k))
+
+    def ig_there(p, k):
+        return send((ia, ib)[p], rg, ig_s.at[8 + k], ig_r, near_plane(k))
 
     def ie_copy(k):
         return send(ie, ree.at[u], ie_s.at[k], ie_r.at[k], plane(k))
 
+    @pl.when(is_a)
+    def _():
+        for p in range(2):
+            loop(1, 8, lambda k, p=p: a_copy(k, p).start())
+        for p in range(2):
+            a_side(p).start()
+        ra[2 * c] = ia[...]
+        ra[2 * c + 1] = ib[...]
+
     for p in range(2):
 
-        @pl.when(z8 == hold(x, c, p))
+        @pl.when(is_g & (c == p))
         def _(p=p):
-            loop(1, 8, lambda k: a_copy(k, 2 * c + p).start())
-            a_side(2 * c + p).start()
-            ra[2 * c + p] = inv_own
-
-    @pl.when(z8 == hold(x, c, 2))
-    def _():
-        loop(1, 8, lambda k: ig_copy(k).start())
-        rg[...] = inv_own
+            loop(0, 8, lambda k: ig_there(1 - p, k).start())
+            loop(1, 8, lambda k: ig_here(p, k).start())
+            rg[...] = (ia, ib)[p][...]
 
     loop(1, 8, lambda k: ie_copy(k).start())
-    ree[u] = inv_e
+    ree[u] = ie[...]
     loop(1, NX, lambda k: g_copy(k).wait_recv())
     rt[x] = gw[:, pl.ds(pl.multiple_of(x * 512, 512), 512)]
 
-    @pl.when(z8 != hold(x, c, 2))
+    @pl.when(jnp.logical_not(is_g))
     def _():
-        ig_copy(1).wait_recv()
+        send(ia, rg, ig_s.at[0], ig_r, other).wait_recv()
 
     pair = rg[...]
     g_block = jnp.where(c == 0, pair[:, :HEAD], pair[:, HEAD:])
     tile = jnp.concatenate([rt[k] for k in range(NX)], axis=0)
     left = jnp.dot(g_block, tile, precision=HI, preferred_element_type=F32)
     for q in range(4):
-        here = z8 == hold(x, q // 2, q % 2)
+        here = z8 == a_place(q // 2)
 
         @pl.when(jnp.logical_not(here) & (c == q % 2))
         def _(q=q):
-            a_side(q).wait_recv()
+            a_came(q)
             a_pass(q).start()
 
     loop(1, 8, lambda k: ie_copy(k).wait_recv())
@@ -417,32 +444,34 @@
         cols = slice(128 * v, 128 * v + 128)
         u_o[:, cols] = jnp.dot(ge[:, cols], blockdiag(ree[v]), precision=HI, preferred_element_type=F32) / row_scale
     for q in range(4):
-        here = z8 == hold(x, q // 2, q % 2)
+        here = z8 == a_place(q // 2)
 
         @pl.when((here & (c != q // 2)) | (jnp.logical_not(here) & (c != q % 2)))
         def _(q=q):
-            a_side(q).wait_recv()
+            a_came(q)
 
         cols = slice(128 * q, 128 * q + 128)
         w_o[:, cols] = jnp.dot(left[:, cols], blockdiag(ra[q]), precision=HI, preferred_element_type=F32)
 
-    for p in range(2):
-
-        @pl.when(z8 == hold(x, c, p))
-        def _(p=p):
-            loop(1, 8, lambda k: a_copy(k, 2 * c + p).wait_send())
-            a_side(2 * c + p).wait_send()
+    @pl.when(is_a)
+    def _():
+        for p in range(2):
+            loop(1, 8, lambda k, p=p: a_copy(k, p).wait_send())
+            a_side(p).wait_send()
 
     for q in range(4):
-        here = z8 == hold(x, q // 2, q % 2)
+        here = z8 == a_place(q // 2)
 
         @pl.when(jnp.logical_not(here) & (c == q % 2))
         def _(q=q):
             a_pass(q).wait_send()
 
-    @pl.when(z8 == hold(x, c, 2))
-    def _():
-        loop(1, 8, lambda k: ig_copy(k).wait_send())
+    for p in range(2):
+
+        @pl.when(is_g & (c == p))
+        def _(p=p):
+            loop(0, 8, lambda k: ig_there(1 - p, k).wait_send())
+            loop(1, 8, lambda k: ig_here(p, k).wait_send())
 
     loop(1, 8, lambda k: ie_copy(k).wait_send())
     e_core.wait_send()
@@ -456,7 +485,7 @@
     loop(1, NY, lambda k: ey_copy(k).wait_send())
     loop(1, NZ, lambda k: n_copy(k).wait_send())
     loop(1, NZ, lambda k: g_out(k).wait_send())
-    for j in range(6):
+    for j in range(3):
         k, copy = z_copy(j)
 
         @pl.when(k != 0)
@@ -475,11 +504,11 @@
 def local(acts, out_cot, emb_ids, emb_cot, grad_w, grad_e):
     dma = pltpu.SemaphoreType.DMA
     buffers = [
-        (2, 24, 64, 128), (2, 64, 128), (4, 24, 128), (64, 128), (64, 128), (8, 128),
-        (24, 64, 128), (64, 128), (4, 24, 128), (24, 64, 128), (16, 4, 128), (4, 24, 128),
-        (16, 8, 128), (4, 128), (4, 128), (6, 64, 128), (4, 6, 64, 128), (16, 4, 128),
-        (16, 24, 128), (4, 4, 128), (16, 64, 128), (16, 8, 128), (16, 4, 128), (4, 16, 512),
-        (64, 128), (64, 128), (4, 64, 128), (64, 128), (8, 64, 128),
+        (2, 4, 200, 128), (2, 64, 128), (4, 24, 128), (72, 128), (64, 128), (8, 128),
+        (4, 200, 128), (64, 128), (4, 24, 128), (4, 200, 128), (16, 4, 128), (4, 24, 128),
+        (16, 8, 128), (4, 128), (4, 128), (3, 72, 128), (4, 200, 128), (16, 4, 128),
+        (16, 24, 128), (4, 4, 128), (16, 72, 128), (16, 8, 128), (16, 4, 128), (4, 16, 512),
+        (64, 128), (64, 128), (64, 128), (4, 64, 128), (64, 128), (8, 64, 128),
     ]
     return pl.pallas_call(
         whole_kernel,
@@ -488,7 +517,7 @@
         out_specs=tuple(vmem(2)),
         scratch_shapes=[pltpu.VMEM(dims, F32) for dims in buffers]
         + [dma((n,)) for n in (6, 6, 4, 4, 16, 16, 16, 16, 4, 4, 6, 16, 16, 16, 16, 16, 4, 4)]
-        + [dma((8,)), dma((4,)), dma((4,)), dma((8,)), dma, dma((8,)), dma((8,))],
+        + [dma((16,)), dma((4,)), dma((4,)), dma((16,)), dma, dma((8,)), dma((8,))],
         compiler_params=pltpu.CompilerParams(collective_id=0, has_side_effects=True),
         name="whole",
     )(acts, out_cot, emb_cot, emb_ids.reshape(1, 64), grad_w, grad_e)

time: 66.5 us -> 60.2 us (0.905)
  the two profiles are of different devices: /device:TPU:1 before, /device:TPU:65 now
where the time goes in v3:
time: 60.2 us; the launch traced here: 60 us
  Pallas kernels  56.4 us (94%)
  local copies, waits for them, and re-layouts  3.04 us (5%)
  between operations  0.64 us (1%)
    pallas_call x1, Pallas kernels, local(): pl.pallas_call(whole_kernel, out_shape=(shape(64, 512), shape(16, 1024)),...  56.4 us
    unnamed x2, local copies, waits for them, and re-layouts  3.04 us

profile of v3, /device:TPU:65, one launch (start us, length us, event | category | flops | bytes accessed | tf_op | source)
XLA Modules:
  0.0 60.0 jit_solution(2227485231798761555)
XLA Ops:
  0.6 56.4 %whole.1 = (f32[64,512]{1,0:T(8,128)}, f32[16,1024]{1,0:T(8,128)}) custom-call(bf16[8,256,512]{2,1,0:T(8,128)(2,1)} %acts.1, bf16[8,256,256]{2,1,0:T(8,128)(2,1)} %cot.1, bf16[256,256]{1,0:T(8,128)(2,1)} %emb.1, s32[1,64]{1,0:T(1,128)} %bitcast.1, f32[16,2048]{1,0:T(8,128)} %gw.1, f32[16,1024]{1,0:T(8,128)} %ge.1), custom_call_target="tpu_custom_call" | custom-call | tf_op jit(solution)/shard_map/whole/pallas_call | solution.py:513
  57.0 1.6 %copy.10 = f32[64,512]{1,0:T(8,128)} copy(f32[64,512]{1,0:T(8,128)} %get-tuple-element.4) | data formatting | bytes 262144
  58.6 1.5 %copy.11 = f32[16,1024]{1,0:T(8,128)} copy(f32[16,1024]{1,0:T(8,128)} %get-tuple-element.5) | data formatting | bytes 131072

commit v4 on v3

--- a/solution.py
+++ b/solution.py
@@ -121,11 +121,10 @@
 def inverses(own, e, tr):
     x, y, z, c = coords()
     sums = trace_sums(tr)
-    low = z < 8
-    ta = jnp.where(low, sums[1:2], sums[2:3])
-    tg = jnp.where(low, sums[3:4], sums[4:5])
+    ta = sums[1:2]
+    tg = sums[2:3]
     ratio = jnp.sqrt((ta / (TOKENS * INNER)) / (tg / (TOKENS * WIDTH)))
-    ratio_e = jnp.sqrt((TOKENS / VOCAB) / (sums[5:6] / (TOKENS * WIDTH)))
+    ratio_e = jnp.sqrt((TOKENS / VOCAB) / (sums[3:4] / (TOKENS * WIDTH)))
     is_g = lax.rem(z, 8) == 2 * x + c
     shift = jnp.where(is_g, DAMP / ratio, DAMP * ratio)
     side = 2 * HEAD
@@ -170,9 +169,9 @@
 def whole_kernel(
     acts, cot, emb, ids_row, gw, ge, w_o, u_o,
     blk, eblk, m, own_v, e_v, tr_v,
-    rblk, reb, rm, s1, se, ms, nz, ec, ef, s2, ry, re, rmm, rey, rz, rn, eag, rt,
+    rblk, reb, rm, s1, sf, se, ms, mx, nz, ec, ef, s2, ry, re, rmy, rmx, rey, rz, rn, eag, rt,
     ia, ib, ie, ra, rg, ree,
-    c_s, c_r, y_s, y_r, e_s, e_r, m_s, m_r, ey_s, ey_r, z_s, z_r, n_s, n_r, g_s, g_r, t_s, t_r,
+    c_s, c_r, y_s, y_r, e_s, e_r, my_s, my_r, mx_s, mx_r, ey_s, ey_r, z_s, z_r, n_s, n_r, g_s, g_r, t_s, t_r,
     a_s, a_r, f_s, ig_s, ig_r, ie_s, ie_r,
 ):
     x, y, z, c = coords()
@@ -184,9 +183,6 @@
     is_g = (z8 == u) & (h == c)
     other = dev(x, y, z, 1 - c)
 
-    def at_xy(k):
-        return lax.rem(x + lax.div(k, 4), 4), lax.rem(y + lax.rem(k, 4), 4)
-
     def at_z(k):
         return dev(x, y, lax.rem(z + k, NZ), c)
 
@@ -200,8 +196,8 @@
     pl.semaphore_signal(barrier, inc=1, device_id=other, device_id_type=MESH)
 
     def greet_xy(k):
-        xx, yy = at_xy(k)
-        pl.semaphore_signal(barrier, inc=1, device_id=dev(xx, yy, z, c), device_id_type=MESH)
+        pl.semaphore_signal(barrier, inc=1, device_id=at_x(k), device_id_type=MESH)
+        pl.semaphore_signal(barrier, inc=1, device_id=at_y(k), device_id_type=MESH)
 
     def greet_z(k):
         pl.semaphore_signal(barrier, inc=1, device_id=at_z(k), device_id_type=MESH)
@@ -213,7 +209,7 @@
     def greet_plane(k):
         pl.semaphore_signal(barrier, inc=1, device_id=dev(lax.rem(x + k, NX), y, z, 1 - c), device_id_type=MESH)
 
-    loop(1, 16, greet_xy)
+    loop(1, 4, greet_xy)
     loop(1, 16, greet_z)
     loop(1, 8, greet_group)
     def greet_near(k):
@@ -223,7 +219,7 @@
     loop(1, NX, greet_plane)
     loop(0, 6, greet_near)
     grams(acts, cot, emb, ids_row, blk, eblk, m)
-    pl.semaphore_wait(barrier, 47)
+    pl.semaphore_wait(barrier, 38)
 
     def core_chunk(i):
         k = (2, 1, 3, 0)[i]
@@ -262,79 +258,55 @@
     for k in range(NY):
         ms[k] = m[k] + rm[k]
 
-    def m_copy(k):
-        xx, yy = at_xy(k)
-        return send(ms.at[yy], rmm.at[k], m_s.at[k], m_r.at[k], dev(xx, yy, z, c))
-
-    def m_start(k):
-        m_copy(k).start()
-
-    loop(1, 16, m_start)
-
-    def y_copy(k):
-        return send(s1.at[lax.rem(y + k, NY)], ry.at[k], y_s.at[k], y_r.at[k], at_y(k))
+    def my_copy(k):
+        return send(ms.at[lax.rem(y + k, NY)], rmy.at[k], my_s.at[k], my_r.at[k], at_y(k))
+
+    def mx_copy(k):
+        return send(mx, rmx.at[k], mx_s.at[k], mx_r.at[k], at_x(k))
+
+    loop(1, NY, lambda k: my_copy(k).start())
+
+    ahead, far, behind = lax.rem(y + 1, NY), lax.rem(y + 2, NY), lax.rem(y + 3, NY)
+    low, high = pl.ds(0, 104), pl.ds(104, 96)
+
+    def y_copy(i):
+        src = (s1.at[far, low], s1.at[far, high], s1.at[ahead, high], s1.at[behind, low], sf.at[low], sf.at[high])[i]
+        dst = (ry.at[0, low], ry.at[0, high], ry.at[1, high], ry.at[2, low], ry.at[1, low], ry.at[2, high])[i]
+        return send(src, dst, y_s.at[i], y_r.at[i], at_y(3 if i % 2 else 1))
 
     for i in range(4):
         k = (2, 1, 3, 0)[i]
         core_chunk(i).wait_recv()
         yy = lax.rem(y + k, NY)
         s1[yy] = blk[c, yy] + rblk[yy]
-        if k:
-            y_copy(k).start()
-
-    def e_add(k, total):
-        e_copy(k).wait_recv()
-        return total + re[k]
-
-    ec[...] = lax.fori_loop(1, NZ, e_add, se[z])
-
-    def ey_copy(k):
-        return send(ec, rey.at[k], ey_s.at[k], ey_r.at[k], at_y(k))
-
-    def ey_start(k):
-        ey_copy(k).start()
-
-    loop(1, NY, ey_start)
-
-    def m_add(k, total):
-        m_copy(k).wait_recv()
-        return total + rmm[k]
-
-    n = lax.fori_loop(1, 16, m_add, ms[y])
-    for k in range(NZ):
-        nz[k] = jnp.concatenate([n[k : k + 1], n[16:23]], axis=0)
-
-    def n_copy(k):
-        return send(nz.at[lax.rem(z + k, NZ)], rn.at[k], n_s.at[k], n_r.at[k], at_z(k))
-
-    def n_start(k):
-        n_copy(k).start()
-
-    loop(1, NZ, n_start)
-
-    def ey_add(k, total):
-        ey_copy(k).wait_recv()
-        return total + rey[k]
-
-    ef[...] = lax.fori_loop(1, NY, ey_add, ec[...])
-
-    def g_out(k):
-        return send(ef, eag.at[z], g_s.at[k], g_r.at[k], at_z(k))
-
-    def g_out_start(k):
-        g_out(k).start()
-
-    loop(1, NZ, g_out_start)
-
-    for k in range(1, NY):
-        y_copy(k).wait_recv()
+        if i == 0:
+            y_copy(0).start()
+            y_copy(1).start()
+        elif i < 3:
+            y_copy(i + 1).start()
+    y_copy(0).wait_recv()
+    sf[0:104] = s1[ahead, 0:104] + ry[0, 0:104]
+    y_copy(4).start()
+    y_copy(1).wait_recv()
+    sf[104:200] = s1[behind, 104:200] + ry[0, 104:200]
+    y_copy(5).start()
+
+    def my_add(k, total):
+        my_copy(k).wait_recv()
+        return total + rmy[k]
+
+    mx[...] = lax.fori_loop(1, NY, my_add, ms[y])
+    loop(1, NX, lambda k: mx_copy(k).start())
+
+    for i in range(2, 6):
+        y_copy(i).wait_recv()
 
     def z_copy(j):
         place = 8 * c + u if j == 2 else 8 * j + a_place(c)
         k = lax.rem(place - z + NZ, NZ)
         return k, send(s2.at[j], rz.at[k], z_s.at[j], z_r.at[k], dev(x, y, place, c))
 
-    chunk = (s1[y] + ry[1]) + (ry[2] + ry[3])
+    chunk = s1[y] + (ry[1] + ry[2])
     for j in range(3):
         s2[j, 0:64] = chunk[64 * j : 64 * j + 64]
         s2[j, 64:72] = jnp.broadcast_to(chunk[192 + j : 193 + j], (8, 128))
@@ -343,6 +315,51 @@
         @pl.when(k != 0)
         def _(copy=copy):
             copy.start()
+
+    def e_add(k, total):
+        e_copy(k).wait_recv()
+        return total + re[k]
+
+    ec[...] = lax.fori_loop(1, NZ, e_add, se[z])
+
+    def ey_copy(k):
+        return send(ec, rey.at[k], ey_s.at[k], ey_r.at[k], at_y(k))
+
+    def ey_start(k):
+        ey_copy(k).start()
+
+    loop(1, NY, ey_start)
+
+    def mx_add(k, total):
+        mx_copy(k).wait_recv()
+        return total + rmx[k]
+
+    n = lax.fori_loop(1, NX, mx_add, mx[...])
+    for k in range(NZ):
+        half = k // 8
+        nz[k] = jnp.concatenate([n[k : k + 1], n[16 + half : 17 + half], n[18 + half : 19 + half], n[20:21]], axis=0)
+
+    def n_copy(k):
+        return send(nz.at[lax.rem(z + k, NZ)], rn.at[k], n_s.at[k], n_r.at[k], at_z(k))
+
+    def n_start(k):
+        n_copy(k).start()
+
+    loop(1, NZ, n_start)
+
+    def ey_add(k, total):
+        ey_copy(k).wait_recv()
+        return total + rey[k]
+
+    ef[...] = lax.fori_loop(1, NY, ey_add, ec[...])
+
+    def g_out(k):
+        return send(ef, eag.at[z], g_s.at[k], g_r.at[k], at_z(k))
+
+    def g_out_start(k):
+        g_out(k).start()
+
+    loop(1, NZ, g_out_start)
 
     def n_add(k, total):
         n_copy(k).wait_recv()
@@ -435,7 +452,7 @@
 
     loop(1, 8, lambda k: ie_copy(k).wait_recv())
     stats = tr_v[...]
-    ratio_e = jnp.sqrt((TOKENS / VOCAB) / (trace_sums(stats)[5:6] / (TOKENS * WIDTH)))
+    ratio_e = jnp.sqrt((TOKENS / VOCAB) / (trace_sums(stats)[3:4] / (TOKENS * WIDTH)))
     lane = lax.broadcasted_iota(jnp.int32, (16, 128), 1)
     row = lax.broadcasted_iota(jnp.int32, (16, 128), 0)
     picked = jnp.where(lane == row + (64 * c + 16 * x), jnp.broadcast_to(stats[0:1], (16, 128)), 0.0)
@@ -480,8 +497,10 @@
         core_chunk(i).wait_send()
     loop(1, NX, lambda k: g_copy(k).wait_send())
     loop(1, NZ, lambda k: e_copy(k).wait_send())
-    loop(1, 16, lambda k: m_copy(k).wait_send())
-    loop(1, NY, lambda k: y_copy(k).wait_send())
+    loop(1, NY, lambda k: my_copy(k).wait_send())
+    loop(1, NX, lambda k: mx_copy(k).wait_send())
+    for i in range(6):
+        y_copy(i).wait_send()
     loop(1, NY, lambda k: ey_copy(k).wait_send())
     loop(1, NZ, lambda k: n_copy(k).wait_send())
     loop(1, NZ, lambda k: g_out(k).wait_send())
@@ -493,6 +512,11 @@
             copy.wait_send()
 
 
+def finish_kernel(w, u, w_o, u_o):
+    w_o[...] = w[...]
+    u_o[...] = u[...]
+
+
 def vmem(count):
     return [pl.BlockSpec(memory_space=pltpu.VMEM)] * count
 
@@ -504,23 +528,30 @@
 def local(acts, out_cot, emb_ids, emb_cot, grad_w, grad_e):
     dma = pltpu.SemaphoreType.DMA
     buffers = [
-        (2, 4, 200, 128), (2, 64, 128), (4, 24, 128), (72, 128), (64, 128), (8, 128),
-        (4, 200, 128), (64, 128), (4, 24, 128), (4, 200, 128), (16, 4, 128), (4, 24, 128),
-        (16, 8, 128), (4, 128), (4, 128), (3, 72, 128), (4, 200, 128), (16, 4, 128),
-        (16, 24, 128), (4, 4, 128), (16, 72, 128), (16, 8, 128), (16, 4, 128), (4, 16, 512),
+        (2, 4, 200, 128), (2, 64, 128), (4, 24, 128), (72, 128), (64, 128), (4, 128),
+        (4, 200, 128), (64, 128), (4, 24, 128), (4, 200, 128), (200, 128), (16, 4, 128), (4, 24, 128), (24, 128),
+        (16, 4, 128), (4, 128), (4, 128), (3, 72, 128), (3, 200, 128), (16, 4, 128),
+        (4, 24, 128), (4, 24, 128), (4, 4, 128), (16, 72, 128), (16, 4, 128), (16, 4, 128), (4, 16, 512),
         (64, 128), (64, 128), (64, 128), (4, 64, 128), (64, 128), (8, 64, 128),
     ]
-    return pl.pallas_call(
+    update_w, update_e = pl.pallas_call(
         whole_kernel,
         out_shape=(shape(64, 512), shape(16, 1024)),
         in_specs=vmem(6),
         out_specs=tuple(vmem(2)),
         scratch_shapes=[pltpu.VMEM(dims, F32) for dims in buffers]
-        + [dma((n,)) for n in (6, 6, 4, 4, 16, 16, 16, 16, 4, 4, 6, 16, 16, 16, 16, 16, 4, 4)]
+        + [dma((n,)) for n in (6, 6, 6, 6, 16, 16, 4, 4, 4, 4, 4, 4, 3, 16, 16, 16, 16, 16, 4, 4)]
         + [dma((16,)), dma((4,)), dma((4,)), dma((16,)), dma, dma((8,)), dma((8,))],
         compiler_params=pltpu.CompilerParams(collective_id=0, has_side_effects=True),
         name="whole",
     )(acts, out_cot, emb_cot, emb_ids.reshape(1, 64), grad_w, grad_e)
+    return pl.pallas_call(
+        finish_kernel,
+        out_shape=(shape(64, 512), shape(16, 1024)),
+        in_specs=vmem(2),
+        out_specs=tuple(vmem(2)),
+        name="finish",
+    )(update_w, update_e)
 
 
 def solution(mesh):

time: 60.2 us -> 57.7 us (0.958)
  the two profiles are of different devices: /device:TPU:65 before, /device:TPU:1 now
where the time goes in v4:
time: 57.7 us; the launch traced here: 57.5 us
  Pallas kernels  56.9 us (99%)
  between operations  0.64 us (1%)
    pallas_call x1, Pallas kernels, local(): pl.pallas_call(whole_kernel, out_shape=(shape(64, 512), shape(16, 1024)),...  55.3 us
    pallas_call x1, Pallas kernels, local(): pl.pallas_call(finish_kernel, out_shape=(shape(64, 512), shape(16, 1024))...  1.59 us

profile of v4, /device:TPU:1, one launch (start us, length us, event | category | flops | bytes accessed | tf_op | source)
XLA Modules:
  0.0 57.5 jit_solution(14005060161666902743)
XLA Ops:
  0.6 55.3 %whole.1 = (f32[64,512]{1,0:T(8,128)}, f32[16,1024]{1,0:T(8,128)}) custom-call(bf16[8,256,512]{2,1,0:T(8,128)(2,1)} %acts.1, bf16[8,256,256]{2,1,0:T(8,128)(2,1)} %cot.1, bf16[256,256]{1,0:T(8,128)(2,1)} %emb.1, s32[1,64]{1,0:T(1,128)} %bitcast.1, f32[16,2048]{1,0:T(8,128)} %gw.1, f32[16,1024]{1,0:T(8,128)} %ge.1), custom_call_target="tpu_custom_call" | custom-call | tf_op jit(solution)/shard_map/whole/pallas_call | solution.py:537
  56.0 1.6 %finish.1 = (f32[64,512]{1,0:T(8,128)}, f32[16,1024]{1,0:T(8,128)}) custom-call(f32[64,512]{1,0:T(8,128)} %get-tuple-element.4.w, f32[16,1024]{1,0:T(8,128)} %get-tuple-element.5.u), custom_call_target="tpu_custom_call" | custom-call | tf_op jit(solution)/shard_map/finish/pallas_call | solution.py:548

commit v5 on v4

--- a/solution.py
+++ b/solution.py
@@ -61,7 +61,7 @@
     return jnp.concatenate([jnp.where(lane < HEAD, pair, zero), jnp.where(lane < HEAD, zero, pair)], axis=0)
 
 
-def grams(acts, cot, emb, ids_row, blk, eblk, m):
+def grams(acts, cot, emb, ids_row, blk, eblk, m, layers):
     lane = lax.broadcasted_iota(jnp.int32, (HEAD, 2 * HEAD), 1)
     row = lax.broadcasted_iota(jnp.int32, (HEAD, 2 * HEAD), 0)
     on_diag = (lane == row) | (lane == row + HEAD)
@@ -90,6 +90,8 @@
     below = {}
     for layer in range(LAYERS):
         y, odd = layer // 2, layer % 2
+        layers[layer][0].wait()
+        layers[layer][1].wait()
         sum_a = jnp.zeros((1, 128), F32)
         sum_g = jnp.zeros((1, 128), F32)
         for core in range(2):
@@ -141,7 +143,7 @@
             jnp.max(jnp.where(top, sums, 0.0), axis=0, keepdims=True),
             jnp.max(jnp.where(top, 0.0, sums), axis=0, keepdims=True),
         )
-        return mat, eye / bound
+        return eye - mat / bound, bound
 
     def fold(mat):
         return mat[:HEAD] + mat[HEAD:]
@@ -153,26 +155,26 @@
     to = jnp.where(to < HEAD, to, to - HEAD)
     first = jnp.where(at <= to, both, turned)
     second = jnp.where(at > to, both, jnp.where(at == to, own[HEAD : HEAD + 1], turned))
-    m0, a0 = start(first, shift)
-    m1, a1 = start(second, shift)
-    m2, a2 = start(e, DAMP / ratio_e)
-    for _ in range(NS_ITERS):
-        i0 = jnp.dot(m0, a0, precision=HI, preferred_element_type=F32)
-        i1 = jnp.dot(m1, a1, precision=HI, preferred_element_type=F32)
-        i2 = jnp.dot(m2, a2, precision=HI, preferred_element_type=F32)
-        a0 = jnp.dot(a0, 2.0 * eye - i0, precision=HI, preferred_element_type=F32)
-        a1 = jnp.dot(a1, 2.0 * eye - i1, precision=HI, preferred_element_type=F32)
-        a2 = jnp.dot(a2, 2.0 * eye - i2, precision=HI, preferred_element_type=F32)
-    return fold(a0), fold(a1), fold(a2)
+    def times(left, right):
+        return [jnp.dot(p, q, precision=HI, preferred_element_type=F32) for p, q in zip(left, right)]
+
+    begun = [start(first, shift), start(second, shift), start(e, DAMP / ratio_e)]
+    power = [rest for rest, _ in begun]
+    product = [eye + rest for rest in power]
+    for _ in range(NS_ITERS - 1):
+        power = times(power, power)
+        product = times(product, [eye + rest for rest in power])
+    return [fold(result / bound) for result, (_, bound) in zip(product, begun)]
 
 
 def whole_kernel(
-    acts, cot, emb, ids_row, gw, ge, w_o, u_o,
+    acts_h, cot_h, emb_h, ids_h, gw_h, ge_h, w_o, u_o,
+    acts, cot, emb, ids_row, gw, ge,
     blk, eblk, m, own_v, e_v, tr_v,
     rblk, reb, rm, s1, sf, se, ms, mx, nz, ec, ef, s2, ry, re, rmy, rmx, rey, rz, rn, eag, rt,
     ia, ib, ie, ra, rg, ree,
     c_s, c_r, y_s, y_r, e_s, e_r, my_s, my_r, mx_s, mx_r, ey_s, ey_r, z_s, z_r, n_s, n_r, g_s, g_r, t_s, t_r,
-    a_s, a_r, f_s, ig_s, ig_r, ie_s, ie_r,
+    a_s, a_r, f_s, ig_s, ig_r, ie_s, ie_r, acts_s, cot_s, in_s,
 ):
     x, y, z, c = coords()
     h = lax.div(z, 8)
@@ -192,6 +194,25 @@
     def at_x(k):
         return dev(lax.rem(x + k, NX), y, z, c)
 
+    small = [
+        pltpu.make_async_copy(src, dst, in_s.at[i])
+        for i, (src, dst) in enumerate([(emb_h, emb), (ids_h, ids_row), (gw_h, gw), (ge_h, ge)])
+    ]
+    small[0].start()
+    small[1].start()
+    layers = [
+        (
+            pltpu.make_async_copy(acts_h.at[l], acts.at[l], acts_s.at[l]),
+            pltpu.make_async_copy(cot_h.at[l], cot.at[l], cot_s.at[l]),
+        )
+        for l in range(LAYERS)
+    ]
+    for first, second in layers:
+        first.start()
+        second.start()
+    small[2].start()
+    small[3].start()
+
     barrier = pltpu.get_barrier_semaphore()
     pl.semaphore_signal(barrier, inc=1, device_id=other, device_id_type=MESH)
 
@@ -218,7 +239,11 @@
 
     loop(1, NX, greet_plane)
     loop(0, 6, greet_near)
-    grams(acts, cot, emb, ids_row, blk, eblk, m)
+    small[0].wait()
+    small[1].wait()
+    grams(acts, cot, emb, ids_row, blk, eblk, m, layers)
+    small[2].wait()
+    small[3].wait()
     pl.semaphore_wait(barrier, 38)
 
     def core_chunk(i):
@@ -537,11 +562,19 @@
     update_w, update_e = pl.pallas_call(
         whole_kernel,
         out_shape=(shape(64, 512), shape(16, 1024)),
-        in_specs=vmem(6),
+        in_specs=[pl.BlockSpec(memory_space=pl.ANY)] * 6,
         out_specs=tuple(vmem(2)),
-        scratch_shapes=[pltpu.VMEM(dims, F32) for dims in buffers]
+        scratch_shapes=[
+            pltpu.VMEM((8, 256, 512), jnp.bfloat16),
+            pltpu.VMEM((8, 256, 256), jnp.bfloat16),
+            pltpu.VMEM((256, 256), jnp.bfloat16),
+            pltpu.VMEM((1, 64), jnp.int32),
+            pltpu.VMEM((16, 2048), F32),
+            pltpu.VMEM((16, 1024), F32),
+        ]
+        + [pltpu.VMEM(dims, F32) for dims in buffers]
         + [dma((n,)) for n in (6, 6, 6, 6, 16, 16, 4, 4, 4, 4, 4, 4, 3, 16, 16, 16, 16, 16, 4, 4)]
-        + [dma((16,)), dma((4,)), dma((4,)), dma((16,)), dma, dma((8,)), dma((8,))],
+        + [dma((16,)), dma((4,)), dma((4,)), dma((16,)), dma, dma((8,)), dma((8,)), dma((8,)), dma((8,)), dma((4,))],
         compiler_params=pltpu.CompilerParams(collective_id=0, has_side_effects=True),
         name="whole",
     )(acts, out_cot, emb_cot, emb_ids.reshape(1, 64), grad_w, grad_e)

time: 57.7 us -> 55.3 us (0.958)
  Pallas kernels: 56.9 us -> 54.5 us
    pallas_call x1, Pallas kernels: 55.3 us -> 52.9 us  [local(): pl.pallas_call(whole_kernel, out_shape=(shape(64, 512), shape(16, 1024)),...]
where the time goes in v5:
time: 55.3 us; the launch traced here: 55.2 us
  Pallas kernels  54.5 us (99%)
  between operations  0.64 us (1%)
    pallas_call x1, Pallas kernels, local(): pl.pallas_call(whole_kernel, out_shape=(shape(64, 512), shape(16, 1024)),...  52.9 us
    pallas_call x1, Pallas kernels, local(): pl.pallas_call(finish_kernel, out_shape=(shape(64, 512), shape(16, 1024))...  1.59 us

profile of v5, /device:TPU:1, one launch (start us, length us, event | category | flops | bytes accessed | tf_op | source)
XLA Modules:
  0.0 55.2 jit_solution(14291660574569712644)
XLA Ops:
  0.6 52.9 %whole.1 = (f32[64,512]{1,0:T(8,128)}, f32[16,1024]{1,0:T(8,128)}) custom-call(bf16[8,256,512]{2,1,0:T(8,128)(2,1)} %acts_h.1, bf16[8,256,256]{2,1,0:T(8,128)(2,1)} %cot_h.1, bf16[256,256]{1,0:T(8,128)(2,1)} %emb_h.1, s32[1,64]{1,0:T(1,128)} %bitcast.1, f32[16,2048]{1,0:T(8,128)} %gw_h.1, f32[16,1024]{1,0:T(8,128)} %ge_h.1), custom_call_target="tpu_custom_call" | custom-call | tf_op jit(solution)/shard_map/whole/pallas_call | solution.py:562
  53.6 1.6 %finish.1 = (f32[64,512]{1,0:T(8,128)}, f32[16,1024]{1,0:T(8,128)}) custom-call(f32[64,512]{1,0:T(8,128)} %get-tuple-element.4.w, f32[16,1024]{1,0:T(8,128)} %get-tuple-element.5.u), custom_call_target="tpu_custom_call" | custom-call | tf_op jit(solution)/shard_map/finish/pallas_call | solution.py:581

commit v6 on v5

--- a/solution.py
+++ b/solution.py
@@ -227,24 +227,20 @@
         near = 8 * h + lax.rem(z8 + k, 8)
         pl.semaphore_signal(barrier, inc=1, device_id=dev(x, y, near, 1 - c), device_id_type=MESH)
 
-    def greet_plane(k):
-        pl.semaphore_signal(barrier, inc=1, device_id=dev(lax.rem(x + k, NX), y, z, 1 - c), device_id_type=MESH)
+    def greet_near(k):
+        near = dev(lax.rem(x + k, NX), y, z_near, c)
+        pl.semaphore_signal(barrier, inc=1, device_id=near, device_id_type=MESH)
 
     loop(1, 4, greet_xy)
     loop(1, 16, greet_z)
     loop(1, 8, greet_group)
-    def greet_near(k):
-        xx = lax.rem(x + 1 + lax.div(k, 2), NX)
-        pl.semaphore_signal(barrier, inc=1, device_id=dev(xx, y, z_near, lax.rem(k, 2)), device_id_type=MESH)
-
-    loop(1, NX, greet_plane)
-    loop(0, 6, greet_near)
+    loop(1, NX, greet_near)
     small[0].wait()
     small[1].wait()
     grams(acts, cot, emb, ids_row, blk, eblk, m, layers)
     small[2].wait()
     small[3].wait()
-    pl.semaphore_wait(barrier, 38)
+    pl.semaphore_wait(barrier, 32)
 
     def core_chunk(i):
         k = (2, 1, 3, 0)[i]
@@ -421,21 +417,31 @@
     def a_pass(q):
         return send(ra.at[q], ra.at[q], f_s.at[q], a_r.at[q], other)
 
-    def plane(k):
-        v = lax.rem(u + k, 8)
-        return dev(lax.div(v, 2), y, z, lax.rem(v, 2))
-
-    def near_plane(k):
-        return dev(lax.div(k, 2), y, z_near, lax.rem(k, 2))
-
     def ig_here(p, k):
-        return send((ia, ib)[p], rg, ig_s.at[k], ig_r, plane(k))
+        return send((ia, ib)[p], rg, ig_s.at[k], ig_r, at_x(k))
 
     def ig_there(p, k):
-        return send((ia, ib)[p], rg, ig_s.at[8 + k], ig_r, near_plane(k))
+        return send((ia, ib)[p], rg, ig_s.at[4 + k], ig_r, dev(k, y, z_near, c))
+
+    def ig_pass():
+        return send(rg, rg, ig_s.at[0], ig_r, other)
+
+    def ig_side(p):
+        return send((ia, ib)[p], rg, ig_s.at[0], ig_r, other)
 
     def ie_copy(k):
-        return send(ie, ree.at[u], ie_s.at[k], ie_r.at[k], plane(k))
+        return send(ie, ree.at[u], ie_s.at[k], ie_r.at[u], at_x(k))
+
+    def ie_side():
+        return send(ie, ree.at[u], ie_s.at[0], ie_r.at[u], other)
+
+    def ie_pass(k):
+        v = 2 * lax.rem(x + k, NX) + c
+        return send(ree.at[v], ree.at[v], ie_s.at[4 + k], ie_r.at[v], other)
+
+    def ie_come(k):
+        v = 2 * lax.rem(x + k, NX) + (1 - c)
+        return send(ie, ree.at[v], ie_s.at[0], ie_r.at[v], other)
 
     @pl.when(is_a)
     def _():
@@ -450,23 +456,28 @@
 
         @pl.when(is_g & (c == p))
         def _(p=p):
-            loop(0, 8, lambda k: ig_there(1 - p, k).start())
-            loop(1, 8, lambda k: ig_here(p, k).start())
+            loop(0, NX, lambda k: ig_there(1 - p, k).start())
+            loop(1, NX, lambda k: ig_here(p, k).start())
+            ig_side(p).start()
             rg[...] = (ia, ib)[p][...]
 
-    loop(1, 8, lambda k: ie_copy(k).start())
+    loop(1, NX, lambda k: ie_copy(k).start())
+    ie_side().start()
     ree[u] = ie[...]
     loop(1, NX, lambda k: g_copy(k).wait_recv())
     rt[x] = gw[:, pl.ds(pl.multiple_of(x * 512, 512), 512)]
 
-    @pl.when(jnp.logical_not(is_g))
+    def ie_forward(k):
+        ie_pass(k).wait_recv()
+        ie_pass(k).start()
+
+    loop(1, NX, ie_forward)
+
+    @pl.when((c == h) & jnp.logical_not(is_g))
     def _():
-        send(ia, rg, ig_s.at[0], ig_r, other).wait_recv()
-
-    pair = rg[...]
-    g_block = jnp.where(c == 0, pair[:, :HEAD], pair[:, HEAD:])
-    tile = jnp.concatenate([rt[k] for k in range(NX)], axis=0)
-    left = jnp.dot(g_block, tile, precision=HI, preferred_element_type=F32)
+        ig_pass().wait_recv()
+        ig_pass().start()
+
     for q in range(4):
         here = z8 == a_place(q // 2)
 
@@ -475,7 +486,7 @@
             a_came(q)
             a_pass(q).start()
 
-    loop(1, 8, lambda k: ie_copy(k).wait_recv())
+    loop(0, NX, lambda k: ie_come(k).wait_recv())
     stats = tr_v[...]
     ratio_e = jnp.sqrt((TOKENS / VOCAB) / (trace_sums(stats)[3:4] / (TOKENS * WIDTH)))
     lane = lax.broadcasted_iota(jnp.int32, (16, 128), 1)
@@ -485,6 +496,15 @@
     for v in range(8):
         cols = slice(128 * v, 128 * v + 128)
         u_o[:, cols] = jnp.dot(ge[:, cols], blockdiag(ree[v]), precision=HI, preferred_element_type=F32) / row_scale
+
+    @pl.when(c != h)
+    def _():
+        ig_pass().wait_recv()
+
+    pair = rg[...]
+    g_block = jnp.where(c == 0, pair[:, :HEAD], pair[:, HEAD:])
+    tile = jnp.concatenate([rt[k] for k in range(NX)], axis=0)
+    left = jnp.dot(g_block, tile, precision=HI, preferred_element_type=F32)
     for q in range(4):
         here = z8 == a_place(q // 2)
 
@@ -512,10 +532,17 @@
 
         @pl.when(is_g & (c == p))
         def _(p=p):
-            loop(0, 8, lambda k: ig_there(1 - p, k).wait_send())
-            loop(1, 8, lambda k: ig_here(p, k).wait_send())
-
-    loop(1, 8, lambda k: ie_copy(k).wait_send())
+            loop(0, NX, lambda k: ig_there(1 - p, k).wait_send())
+            loop(1, NX, lambda k: ig_here(p, k).wait_send())
+            ig_side(p).wait_send()
+
+    @pl.when((c == h) & jnp.logical_not(is_g))
+    def _():
+        ig_pass().wait_send()
+
+    loop(1, NX, lambda k: ie_copy(k).wait_send())
+    ie_side().wait_send()
+    loop(1, NX, lambda k: ie_pass(k).wait_send())
     e_core.wait_send()
     m_core.wait_send()
     for i in range(4):

time: 55.3 us -> 56.2 us (1.016)
  Pallas kernels: 54.5 us -> 55.4 us
    pallas_call x1, Pallas kernels: 52.9 us -> 53.8 us  [local(): pl.pallas_call(whole_kernel, out_shape=(shape(64, 512), shape(16, 1024)),...]
where the time goes in v6:
time: 56.2 us; the launch traced here: 56.1 us
  Pallas kernels  55.4 us (99%)
  between operations  0.64 us (1%)
    pallas_call x1, Pallas kernels, local(): pl.pallas_call(whole_kernel, out_shape=(shape(64, 512), shape(16, 1024)),...  53.8 us
    pallas_call x1, Pallas kernels, local(): pl.pallas_call(finish_kernel, out_shape=(shape(64, 512), shape(16, 1024))...  1.59 us

profile of v6, /device:TPU:1, one launch (start us, length us, event | category | flops | bytes accessed | tf_op | source)
XLA Modules:
  0.0 56.1 jit_solution(2848427034225068610)
XLA Ops:
  0.6 53.8 %whole.1 = (f32[64,512]{1,0:T(8,128)}, f32[16,1024]{1,0:T(8,128)}) custom-call(bf16[8,256,512]{2,1,0:T(8,128)(2,1)} %acts_h.1, bf16[8,256,256]{2,1,0:T(8,128)(2,1)} %cot_h.1, bf16[256,256]{1,0:T(8,128)(2,1)} %emb_h.1, s32[1,64]{1,0:T(1,128)} %bitcast.1, f32[16,2048]{1,0:T(8,128)} %gw_h.1, f32[16,1024]{1,0:T(8,128)} %ge_h.1), custom_call_target="tpu_custom_call" | custom-call | tf_op jit(solution)/shard_map/whole/pallas_call | solution.py:589
  54.5 1.6 %finish.1 = (f32[64,512]{1,0:T(8,128)}, f32[16,1024]{1,0:T(8,128)}) custom-call(f32[64,512]{1,0:T(8,128)} %get-tuple-element.4.w, f32[16,1024]{1,0:T(8,128)} %get-tuple-element.5.u), custom_call_target="tpu_custom_call" | custom-call | tf_op jit(solution)/shard_map/finish/pallas_call | solution.py:608

commit v7 on v6

--- a/solution.py
+++ b/solution.py
@@ -33,7 +33,7 @@
 
 
 def a_place(core):
-    return 3 + core
+    return 5 - 3 * core
 
 
 def send(src, dst, send_sem, recv_sem, device):

time: 56.2 us -> 54.8 us (0.975)
  Pallas kernels: 55.4 us -> 54.1 us
    pallas_call x1, Pallas kernels: 53.8 us -> 52.5 us  [local(): pl.pallas_call(whole_kernel, out_shape=(shape(64, 512), shape(16, 1024)),...]
where the time goes in v7:
time: 54.8 us; the launch traced here: 54.7 us
  Pallas kernels  54.1 us (99%)
  between operations  0.64 us (1%)
    pallas_call x1, Pallas kernels, local(): pl.pallas_call(whole_kernel, out_shape=(shape(64, 512), shape(16, 1024)),...  52.5 us
    pallas_call x1, Pallas kernels, local(): pl.pallas_call(finish_kernel, out_shape=(shape(64, 512), shape(16, 1024))...  1.59 us

profile of v7, /device:TPU:1, one launch (start us, length us, event | category | flops | bytes accessed | tf_op | source)
XLA Modules:
  0.0 54.7 jit_solution(7722581870894422939)
XLA Ops:
  0.6 52.5 %whole.1 = (f32[64,512]{1,0:T(8,128)}, f32[16,1024]{1,0:T(8,128)}) custom-call(bf16[8,256,512]{2,1,0:T(8,128)(2,1)} %acts_h.1, bf16[8,256,256]{2,1,0:T(8,128)(2,1)} %cot_h.1, bf16[256,256]{1,0:T(8,128)(2,1)} %emb_h.1, s32[1,64]{1,0:T(1,128)} %bitcast.1, f32[16,2048]{1,0:T(8,128)} %gw_h.1, f32[16,1024]{1,0:T(8,128)} %ge_h.1), custom_call_target="tpu_custom_call" | custom-call | tf_op jit(solution)/shard_map/whole/pallas_call | solution.py:589
  53.1 1.6 %finish.1 = (f32[64,512]{1,0:T(8,128)}, f32[16,1024]{1,0:T(8,128)}) custom-call(f32[64,512]{1,0:T(8,128)} %get-tuple-element.4.w, f32[16,1024]{1,0:T(8,128)} %get-tuple-element.5.u), custom_call_target="tpu_custom_call" | custom-call | tf_op jit(solution)/shard_map/finish/pallas_call | solution.py:608
